TPU v7x, 256 devices: a whole 4x4x8 slice. The times are simulated.
256 devices in a mesh: owner: 8 (over y, core), group: 32 (over z, x).
Axes of the slice: x: 4, y: 4, z: 8, core: 2. Of those that a mesh axis runs over, the one named last changes fastest.
Arguments:
- amplitudes: bfloat16 [1024, 32768], P('group', 'owner'), may hold values from -6 to 6
- integrals: bfloat16 [32768, 32768], P('owner', 'group'), may hold values from -0.09375 to 0.09375
- occ_irrep: int32 [100], replicated, may hold values from 0 to 7
- vir_irrep: int32 [1200], replicated, may hold values from 0 to 7, as said below
- cd_list: int32 [2, 32768], P(None, 'owner'), may hold values from 0 to 1199
- ab_list: int32 [2, 32768], P(None, 'group'), may hold values from 0 to 1199, as said below
Outputs:
- ladder: bfloat16 [1024, 32768], P('owner', 'group')
Inputs may be any that keep to these rules, and one draw needn't show every extreme that they name: `vir_irrep`: irrep labels of D2h; each of the 8 labels occurs. `occ_irrep`: irrep labels of D2h. `cd_list`: indices of virtual orbitals. `ab_list`: indices of virtual orbitals; the residual pairs of each index of group form 8 consecutive blocks of 128 pairs, and every pair (a,b) of block k has vir_irrep[a] XOR vir_irrep[b] == k.
All inputs are finite; a program needn't handle non-finite values.
Results may differ from a plain program's by a relative error of at most 0.001.
Values may be sent and summed in bfloat16 or wider, within the bound.
No kernel may reach another device: no remote copies, remote signals or barrier semaphores. Data moves between devices by JAX's collectives and lax.ppermute only.
A program may use at most 64 MiB of HBM per device.

v0:
```python
import functools

import jax
import jax.numpy as jnp
from jax import lax
from jax.experimental import pallas as pl
from jax.experimental.pallas import tpu as pltpu
from jax.sharding import Mesh, PartitionSpec as P


LANES = 128
CLASSES = 8
SLOTS = 640
CHUNK, WINDOW = 1024, 256
F32, BF16, I32 = jnp.float32, jnp.bfloat16, jnp.int32
VMEM = pl.BlockSpec(memory_space=pltpu.VMEM)
SMEM = pl.BlockSpec(memory_space=pltpu.SMEM)
ANY = pl.BlockSpec(memory_space=pl.ANY)
WIDTH = 256


def iota(shape, dim):
    return lax.broadcasted_iota(I32, shape, dim)


def row_classes(occ_row, first, rows, n_occ):
    r = first + iota((rows, LANES), 0)
    i = jnp.zeros_like(r)
    for m in range(1, 11):
        i = i + (r >= m * n_occ).astype(I32)
    j = r - i * n_occ
    lane = iota((rows, LANES), 1)
    occ = jnp.broadcast_to(occ_row, (rows, LANES))
    a = jnp.sum(jnp.where(lane == i, occ, 0), axis=1, keepdims=True)
    b = jnp.sum(jnp.where(lane == j, occ, 0), axis=1, keepdims=True)
    return jnp.bitwise_xor(a, b)


def pack_kernel(
    n_occ, n_vir, start, occ_ref, vir_ref, cd_ref, amp_ref, w_ref,
    t_ref, hot_ref, slot_ref, symt_ref, cnt_ref, win_ref, next_ref, occ_s, vir_s, idx_s, acc, kept, sem
):
    load = quarter(w_ref, next_ref, 0, sem)
    rows, pairs = amp_ref.shape
    chunks = pairs // LANES
    occ_s[...] = jnp.zeros_like(occ_s)
    occ_s[:, :n_occ] = occ_ref[...]
    vir_s[...] = jnp.zeros_like(vir_s)
    vir_s[:, :n_vir] = vir_ref[...].reshape(1, n_vir)
    for m in range(chunks):
        for k in range(2):
            idx_s[k * chunks + m : k * chunks + m + 1, :] = cd_ref[k : k + 1, m * LANES : (m + 1) * LANES]
    words = []
    for w in range(2):
        word = jnp.zeros((1, LANES), I32)
        for k in range(8):
            at = (w * 8 + k) * LANES
            if at < n_vir:
                word = word | (vir_s[:, at : at + LANES] << (4 * k))
        words.append(word)
    idx = idx_s[...]
    low, high = idx & (LANES - 1), idx >> 7
    found = [
        jnp.take_along_axis(jnp.broadcast_to(w, idx.shape), low, axis=1, mode="promise_in_bounds") for w in words
    ]
    label = lax.shift_right_logical(jnp.where(high < 8, found[0], found[1]), (high & 7) * 4) & 7
    sym = jnp.bitwise_xor(label[:chunks], label[chunks:])

    hot = jnp.concatenate([(sym == g).astype(F32) for g in range(CLASSES)], axis=0).astype(BF16)
    before = (iota((LANES, LANES), 0) < iota((LANES, LANES), 1)).astype(F32).astype(BF16)
    inside = jnp.dot(hot, before, preferred_element_type=F32)
    total = jnp.dot(hot, jnp.ones((LANES, LANES), BF16), preferred_element_type=F32)
    earlier = (iota((chunks, chunks), 1) < iota((chunks, chunks), 0)).astype(F32).astype(BF16)
    slot = jnp.zeros((chunks, LANES), F32)
    first = jnp.full((chunks, LANES), 2.0 * pairs, F32)
    last = jnp.zeros((chunks, LANES), F32)
    for g in range(CLASSES):
        part = slice(g * chunks, (g + 1) * chunks)
        base = jnp.dot(earlier, total[part].astype(BF16), preferred_element_type=F32)
        slot = jnp.where(sym == g, inside[part] + base, slot)
        first = jnp.minimum(first, base)
        last = jnp.maximum(last, base + total[part])
    cnt_ref[...] = jnp.broadcast_to(last[chunks - 1 :, :], cnt_ref.shape)
    slot = slot.astype(I32) - start[0]
    slot_ref[...] = slot
    wide = jnp.concatenate([sym, jnp.zeros((LANES - chunks, LANES), I32)], axis=0).astype(F32)
    symt_ref[...] = wide.T

    gidx = lax.axis_index("z") * 4 + lax.axis_index("x")
    cls = row_classes(occ_s[...], gidx * rows, rows, n_occ)
    acc[...] = jnp.zeros_like(acc)
    per = CHUNK // LANES

    def place(kept, one, low):
        out = lax.dot_general(kept, one, (((1,), (1,)), ((), ())), preferred_element_type=F32)
        out = jnp.concatenate([out, jnp.zeros((rows, LANES), F32)], axis=1)
        at = pl.ds(pl.multiple_of(low // LANES * LANES, LANES), WINDOW + LANES)
        acc[:, at] += pltpu.roll(out, lax.rem(low, LANES), axis=1)

    lows = []
    for c in range(pairs // CHUNK):
        low = jnp.max(first[c * per : c * per + 1]).astype(I32) - start[0]
        high = jnp.max(last[(c + 1) * per - 1 : (c + 1) * per]).astype(I32) - start[0]
        low = jnp.clip(low, 0, SLOTS - 16) // 16 * 16
        lows.append((low, (jnp.minimum(high, SLOTS) - low + WINDOW - 1) // WINDOW))
    for c, (low, windows) in enumerate(lows):
        win_ref[2 * c] = low
        win_ref[2 * c + 1] = windows
        amp = amp_ref[:, c * CHUNK : (c + 1) * CHUNK].astype(F32)
        kept[:, c * CHUNK : (c + 1) * CHUNK] = jnp.where(cls == lines(sym, c, per), amp, 0.0).astype(BF16)
        one = one_hot(lines(slot, c, per), low)
        hot_ref[c] = one
        place(kept[:, c * CHUNK : (c + 1) * CHUNK], one, low)
    for c, (low, windows) in enumerate(lows):

        @pl.loop(1, windows)
        def _(i):
            at = low + i * WINDOW
            place(kept[:, c * CHUNK : (c + 1) * CHUNK], one_hot(lines(slot_ref[...], c, per), at), at)

    t_ref[...] = acc[:, :SLOTS].astype(BF16)
    load.wait()


def lines(a, c, per):
    return jnp.concatenate([a[c * per + i : c * per + i + 1] for i in range(per)], axis=1)


def one_hot(line, low):
    return (iota((WINDOW, CHUNK), 0) == line - low).astype(F32).astype(BF16)


def quarter(w_ref, into, part, sem):
    copy = pltpu.make_async_copy(w_ref.at[:, part * WIDTH : (part + 1) * WIDTH], into, sem)
    copy.start()
    return copy


def weights_kernel(part, more, win, hot_ref, slot_ref, symt_ref, ready_ref, *refs):
    if more:
        w_ref, out_ref, next_ref, kept, acc, sem = refs
        load = quarter(w_ref, next_ref, part + 1, sem)
    else:
        out_ref, kept, acc = refs
    width = out_ref.shape[1]
    per = CHUNK // LANES
    acc[...] = jnp.zeros_like(acc)
    for c in range(ready_ref.shape[0] // CHUNK):
        for m in range(per):
            sym = jnp.broadcast_to(symt_ref[:, c * per + m : c * per + m + 1], (LANES, LANES)).astype(BF16)
            rows = slice(c * CHUNK + m * LANES, c * CHUNK + (m + 1) * LANES)
            for q in range(width // LANES):
                g = part * (width // LANES) + q
                w = ready_ref[rows, q * LANES : (q + 1) * LANES]
                kept[m * LANES : (m + 1) * LANES, q * LANES : (q + 1) * LANES] = jnp.where(sym == BF16(g), w, BF16(0))
        low = win[2 * c]
        at = pl.ds(pl.multiple_of(low, 16), WINDOW)
        acc[at, :] += jnp.dot(hot_ref[c], kept[...], preferred_element_type=F32)

        @pl.loop(1, win[2 * c + 1])
        def _(i):
            at = pl.multiple_of(low + i * WINDOW, 16)
            one = one_hot(lines(slot_ref[...], c, per), at)
            acc[pl.ds(at, WINDOW), :] += jnp.dot(one, kept[...], preferred_element_type=F32)

    out_ref[...] = acc[:SLOTS].astype(BF16)
    if more:
        load.wait()


def multiply(n_occ, places, occ_ref, blocks, weights, out, occ_s):
    z, x = lax.axis_index("z"), lax.axis_index("x")
    occ_s[...] = jnp.zeros_like(occ_s)
    occ_s[:, :n_occ] = occ_ref[...]
    for ref, (dz, order) in zip(blocks, places):
        height = ref.shape[0]
        owner = (z + dz) % 8
        total = jnp.zeros((height, LANES), F32)
        piece = height // len(order)
        starts = [owner * height + (x + dx) % 4 * piece for dx in order]
        cls = jnp.concatenate([row_classes(occ_s[...], at, piece, n_occ) for at in starts], axis=0)
        for p, w in enumerate(weights):
            part = jnp.dot(ref[...], w[...], preferred_element_type=F32)
            for q in range(w.shape[1] // LANES):
                g = p * (w.shape[1] // LANES) + q
                total = total + jnp.where(cls == g, part[:, q * LANES : (q + 1) * LANES], 0.0)
        for j, dx in enumerate(order):
            at = pl.ds(pl.multiple_of((x + dx) % 4 * piece, piece), piece)
            out[owner, at] = total[j * piece : (j + 1) * piece]


def early_kernel(n_occ, places, occ_ref, *refs):
    n = len(places)
    sums_ref, occ_s = refs[-2:]
    multiply(n_occ, places, occ_ref, refs[:n], refs[n:-2], sums_ref, occ_s)


def product_kernel(n_occ, places, occ_ref, cnt_ref, early_ref, *refs):
    n = len(places)
    keep_ref, send_ref, sums_s, occ_s = refs[-4:]
    multiply(n_occ, places, occ_ref, refs[:n], refs[n:-4], sums_s, occ_s)
    core, z = lax.axis_index("core"), lax.axis_index("z")
    late = (z + places[0][0]) % 8
    for ref, odd in ((keep_ref, core), (send_ref, 1 - core)):
        for k in range(4):
            owner = 2 * k + odd

            @pl.when(owner != late)
            def _():
                ref[k, :128] = early_ref[owner]

            @pl.when(owner == late)
            def _():
                ref[k, :128] = sums_s[owner]

            ref[k, 128:] = cnt_ref[...]


def fold_kernel(keep_ref, got_ref, *outs):
    y = lax.axis_index("y")
    for k, out in enumerate(outs):
        at = (y + k) % 4
        out[:128] = keep_ref[at, :128] + got_ref[at, :128]
        out[128:] = jnp.maximum(keep_ref[at, 128:], got_ref[at, 128:])


def finish_kernel(n_occ, occ_ref, prev_ref, a, b, c, d, out_ref, sum_ref, most_ref, occ_s):
    first = (lax.axis_index("y") * 2 + lax.axis_index("core")) * 128
    occ_s[...] = jnp.zeros_like(occ_s)
    occ_s[:, :n_occ] = occ_ref[...]
    cls = row_classes(occ_s[...], first, 128, n_occ)
    total = (a[:128] + b[:128]) + (c[:128] + d[:128])
    if prev_ref is not None:
        total = total + prev_ref[...]
    sum_ref[...] = total
    most = jnp.maximum(jnp.maximum(a[128:], b[128:]), jnp.maximum(c[128:], d[128:]))
    most_ref[0] = jnp.max(most).astype(I32)
    for g in range(CLASSES):
        out_ref[:, g * LANES : (g + 1) * LANES] = jnp.where(cls == g, total, 0.0).astype(BF16)


def params(mib):
    return pltpu.CompilerParams(vmem_limit_bytes=mib << 20)


def cost(flops, nbytes):
    return pl.CostEstimate(flops=flops, bytes_accessed=nbytes, transcendentals=0)


def shift(a, axis, size, k):
    return lax.ppermute(a, axis, [(i, (i + k) % size) for i in range(size)])


def round_body(start, prev, amplitudes, integrals, occ_irrep, vir_irrep, cd_list):
    n_occ, n_vir = occ_irrep.shape[0], vir_irrep.shape[0]
    rows, pairs = amplitudes.shape
    cols = integrals.shape[1]
    sds = jax.ShapeDtypeStruct
    occ = occ_irrep.reshape(1, n_occ)
    packed, hot, slot, symt, most, win, ready = pl.pallas_call(
        functools.partial(pack_kernel, n_occ, n_vir),
        out_shape=(
            sds((rows, SLOTS), BF16),
            sds((pairs // CHUNK, WINDOW, CHUNK), BF16),
            sds((pairs // LANES, LANES), I32),
            sds((LANES, LANES), F32),
            sds((8, LANES), F32),
            sds((2 * pairs // CHUNK,), I32),
            pltpu.VMEM((pairs, WIDTH), BF16),
        ),
        in_specs=[SMEM, VMEM, VMEM, VMEM, VMEM, ANY],
        out_specs=(VMEM,) * 5 + (SMEM, VMEM),
        scratch_shapes=[
            pltpu.VMEM((1, LANES), I32),
            pltpu.VMEM((1, 10 * LANES), I32),
            pltpu.VMEM((2 * pairs // LANES, LANES), I32),
            pltpu.VMEM((rows, SLOTS + 3 * LANES), F32),
            pltpu.VMEM((rows, pairs), BF16),
            pltpu.SemaphoreType.DMA,
        ],
        compiler_params=params(8),
        cost_estimate=cost(2 * rows * pairs * SLOTS, 6 << 20),
        name="pack",
    )(start, occ, vir_irrep, cd_list, amplitudes, integrals)

    parts = []
    count = cols // WIDTH
    for k in range(count):
        more = k + 1 < count
        out = (sds((SLOTS, WIDTH), BF16),) + more * (pltpu.VMEM((pairs, WIDTH), BF16),)
        scratch = [pltpu.VMEM((CHUNK, WIDTH), BF16), pltpu.VMEM((SLOTS + WINDOW, WIDTH), F32)]
        part, *ready = pl.pallas_call(
            functools.partial(weights_kernel, k, more),
            out_shape=out,
            in_specs=[SMEM, VMEM, VMEM, VMEM, VMEM] + more * [ANY],
            out_specs=(VMEM,) * len(out),
            scratch_shapes=scratch + more * [pltpu.SemaphoreType.DMA],
            compiler_params=params(16),
            cost_estimate=cost(2 * WIDTH * pairs * SLOTS, 7 << 20),
            name="weights",
        )(win, hot, slot, symt, ready, *(more * (integrals,)))
        parts.append(part)
        ready = ready[0] if more else None

    near = [packed] + [shift(packed, "x", 4, k) for k in (2, 1, 3)]
    order = (0, 2, 3, 1)
    mine = jnp.concatenate(near, axis=0)
    blocks, places = [mine], [(0, order)]
    up = down = mine
    for k in range(1, 5):
        up = shift(up, "z", 8, 1)
        blocks.append(up)
        places.append((8 - k, order))
        if k < 4:
            down = shift(down, "z", 8, 7)
            blocks.append(down)
            places.append((k, order))

    sums = sds((8, 128, LANES), F32)
    early = pl.pallas_call(
        functools.partial(early_kernel, n_occ, places[:-1]),
        out_shape=sums,
        in_specs=[VMEM] * (len(blocks) + len(parts)),
        out_specs=VMEM,
        scratch_shapes=[pltpu.VMEM((1, LANES), I32)],
        compiler_params=params(8),
        cost_estimate=cost(2 * 896 * cols * SLOTS, 4 << 20),
        name="early",
    )(occ, *blocks[:-1], *parts)
    keep, send = pl.pallas_call(
        functools.partial(product_kernel, n_occ, places[-1:]),
        out_shape=(sds((4, 136, LANES), F32),) * 2,
        in_specs=[VMEM] * (4 + len(parts)),
        out_specs=(VMEM,) * 2,
        scratch_shapes=[pltpu.VMEM((8, 128, LANES), F32), pltpu.VMEM((1, LANES), I32)],
        compiler_params=params(8),
        cost_estimate=cost(2 * 128 * cols * SLOTS, 1 << 20),
        name="product",
    )(occ, most, early, blocks[-1], *parts)

    got = shift(send, "core", 2, 1)
    folded = pl.pallas_call(
        fold_kernel,
        out_shape=(sds((136, LANES), F32),) * 4,
        in_specs=[VMEM] * 2,
        out_specs=(VMEM,) * 4,
        compiler_params=params(8),
        name="fold",
    )(keep, got)
    arrived = [folded[0]] + [shift(folded[k], "y", 4, k) for k in (2, 1, 3)]
    kernel = functools.partial(finish_kernel, n_occ)
    if prev is None:
        kernel = lambda occ_ref, *refs: finish_kernel(n_occ, occ_ref, None, *refs)
    extra = () if prev is None else (prev,)
    return pl.pallas_call(
        kernel,
        out_shape=(sds((128, cols), BF16), sds((128, LANES), F32), sds((1,), I32)),
        in_specs=[VMEM] * (5 + len(extra)),
        out_specs=(VMEM, VMEM, SMEM),
        scratch_shapes=[pltpu.VMEM((1, LANES), I32)],
        compiler_params=params(8),
        name="finish",
    )(occ, *extra, *arrived)


def local(amplitudes, integrals, occ_irrep, vir_irrep, cd_list, ab_list):
    args = (amplitudes, integrals, occ_irrep, vir_irrep, cd_list)
    out, total, most = round_body(jnp.zeros((1,), I32), None, *args)

    def more(out, total, most):
        def body(state):
            k, _, total = state
            out, total, _ = round_body((k * SLOTS).reshape(1), total, *args)
            return k + 1, out, total

        return lax.while_loop(lambda s: s[0] * SLOTS < most[0], body, (jnp.int32(1), out, total))[1]

    return lax.cond(most[0] > SLOTS, more, lambda out, total, most: out, out, total, most)


def solution(mesh):
    fine = Mesh(mesh.devices.reshape(4, 2, 8, 4), ("y", "core", "z", "x"))
    owner, group = ("y", "core"), ("z", "x")
    return jax.shard_map(
        local,
        mesh=fine,
        in_specs=(P(group, owner), P(owner, group), P(), P(), P(None, owner), P(None, group)),
        out_specs=P(owner, group),
        check_vma=False,
    )
```

profile of v0, /device:TPU:30, one launch (start us, length us, event | category | flops | bytes accessed | tf_op | source)
XLA Modules:
  0.0 57.4 jit_solution(14872175862549354146)
XLA Ops:
  0.0 4.7 %pack.2 = (bf16[32,640]{1,0:T(8,128)(2,1)S(1)}, bf16[4,256,1024]{2,1,0:T(8,128)(2,1)S(1)}, s32[32,128]{1,0:T(8,128)S(1)}, f32[128,128]{1,0:T(8,128)S(1)}, f32[8,...) custom-call(s32[1]{0:T(128)} %constant.7.clone.1.start, s32[1,100]{1,0:T(1,128)} %bitcast.10, ...), custom_call_target="tpu_custom_call" | custom-call | flops 167772160 | bytes 6291456 | tf_op jit(solution)/shard_map/pack/pallas_call | solution.py:260
  4.7 1.5 %collective-permute-start.14 = (bf16[32,640]{1,0:T(8,128)(2,1)S(1)}, bf16[32,640]{1,0:T(8,128)(2,1)S(1)}, u32[]{:S(2)}, u32[]{:S(2)}) collective-permute-start(bf16[32,640]{1,0:T(8,128)(2,1)S(1)} %get-tuple-element.124), channel_id=1, source_target_pairs={{0,2},{1,3},{2,0},{3,1},{4,6},{5,7},{6,4},{7,5},{8,10},{9,11},{10,... | collective-permute-start | bytes 122888 | tf_op jit(solution)/shard_map/ppermute | solution.py:251
  6.2 2.1 %collective-permute-start.15 = (bf16[32,640]{1,0:T(8,128)(2,1)S(1)}, bf16[32,640]{1,0:T(8,128)(2,1)S(1)}, u32[]{:S(2)}, u32[]{:S(2)}) collective-permute-start(bf16[32,640]{1,0:T(8,128)(2,1)S(1)} %get-tuple-element.124), channel_id=1, source_target_pairs={{0,1},{1,2},{2,3},{3,0},{4,5},{5,6},{6,7},{7,4},{8,9},{9,10},{10,1... | collective-permute-start | bytes 122888 | tf_op jit(solution)/shard_map/ppermute | solution.py:251
  8.3 2.1 %collective-permute-done.14 = bf16[32,640]{1,0:T(8,128)(2,1)S(1)} collective-permute-done((bf16[32,640]{1,0:T(8,128)(2,1)S(1)}, bf16[32,640]{1,0:T(8,128)(2,1)S(1)}, u32[]{:S(2)}, u32[]{:S(2)}) %collective-permute-start.14) | collective-permute-done | bytes 40992 | tf_op jit(solution)/shard_map/ppermute | solution.py:251
  10.4 3.1 %collective-permute-done.16 = bf16[32,640]{1,0:T(8,128)(2,1)S(1)} collective-permute-done((bf16[32,640]{1,0:T(8,128)(2,1)S(1)}, bf16[32,640]{1,0:T(8,128)(2,1)S(1)}, u32[]{:S(2)}, u32[]{:S(2)}) %collective-permute-start.16) | collective-permute-done | bytes 40992 | tf_op jit(solution)/shard_map/ppermute | solution.py:251
  13.5 1.9 %collective-permute-start.17 = (bf16[128,640]{1,0:T(8,128)(2,1)S(1)}, bf16[128,640]{1,0:T(8,128)(2,1)S(1)}, u32[]{:S(2)}, u32[]{:S(2)}) collective-permute-start(bf16[128,640]{1,0:T(8,128)(2,1)S(1)} %constant_dynamic-update-slice_fusion.4.refs_0_), channel_id=1, source_target_pairs={{0,4},{4,8},{8,12},{12,16},{16,20},{20,24},{24,28},{28,0},{1,5},{5... | collective-permute-start | bytes 491528 | tf_op jit(solution)/shard_map/ppermute | solution.py:251
  15.4 4.0 %collective-permute-start.18 = (bf16[128,640]{1,0:T(8,128)(2,1)S(1)}, bf16[128,640]{1,0:T(8,128)(2,1)S(1)}, u32[]{:S(2)}, u32[]{:S(2)}) collective-permute-start(bf16[128,640]{1,0:T(8,128)(2,1)S(1)} %constant_dynamic-update-slice_fusion.4.refs_0_), channel_id=1, source_target_pairs={{0,28},{4,0},{8,4},{12,8},{16,12},{20,16},{24,20},{28,24},{1,29},{... | collective-permute-start | bytes 491528 | tf_op jit(solution)/shard_map/ppermute | solution.py:251
  19.4 3.2 %collective-permute-done.17.refs_1_ = bf16[128,640]{1,0:T(8,128)(2,1)S(1)} collective-permute-done((bf16[128,640]{1,0:T(8,128)(2,1)S(1)}, bf16[128,640]{1,0:T(8,128)(2,1)S(1)}, u32[]{:S(2)}, u32[]{:S(2)}) %collective-permute-start.17) | collective-permute-done | bytes 163872 | tf_op jit(solution)/shard_map/ppermute | solution.py:251
  22.7 3.3 %collective-permute-start.20 = (bf16[128,640]{1,0:T(8,128)(2,1)S(1)}, bf16[128,640]{1,0:T(8,128)(2,1)S(1)}, u32[]{:S(2)}, u32[]{:S(2)}) collective-permute-start(bf16[128,640]{1,0:T(8,128)(2,1)S(1)} %collective-permute-done.18.refs_2_), channel_id=1, source_target_pairs={{0,28},{4,0},{8,4},{12,8},{16,12},{20,16},{24,20},{28,24},{1,29},{... | collective-permute-start | bytes 491528 | tf_op jit(solution)/shard_map/ppermute | solution.py:251
  26.0 2.3 %weights.8 = (bf16[640,256]{1,0:T(8,128)(2,1)S(1)}, bf16[4096,256]{1,0:T(8,128)(2,1)S(1)}) custom-call(s32[8]{0:T(128)S(1)} %get-tuple-element.125.win, bf16[4,256,1024]{2,1,0:T(8,128)(2,1)S(1)} %get-tuple-element.126.hot_ref, s32[32,128]{1,0:T(8,128)S(1)} %get-tuple-element.127.slot_ref, f32[128,128]{1,0:T(8,128)S(1)} %get-tuple-element.128.symt_ref, ...), custom_call_target="tpu_custom_call" | custom-call | flops 1342177280 | bytes 7340032 | tf_op jit(solution)/shard_map/weights/pallas_call | solution.py:292
  28.3 1.0 %collective-permute-done.19.refs_3_ = bf16[128,640]{1,0:T(8,128)(2,1)S(1)} collective-permute-done((bf16[128,640]{1,0:T(8,128)(2,1)S(1)}, bf16[128,640]{1,0:T(8,128)(2,1)S(1)}, u32[]{:S(2)}, u32[]{:S(2)}) %collective-permute-start.19) | collective-permute-done | bytes 163872 | tf_op jit(solution)/shard_map/ppermute | solution.py:251
  29.3 2.6 %weights.9 = (bf16[640,256]{1,0:T(8,128)(2,1)S(1)}, bf16[4096,256]{1,0:T(8,128)(2,1)S(1)}) custom-call(s32[8]{0:T(128)S(1)} %get-tuple-element.125.win, bf16[4,256,1024]{2,1,0:T(8,128)(2,1)S(1)} %get-tuple-element.126.hot_ref, s32[32,128]{1,0:T(8,128)S(1)} %get-tuple-element.127.slot_ref, f32[128,128]{1,0:T(8,128)S(1)} %get-tuple-element.128.symt_ref, ...), custom_call_target="tpu_custom_call" | custom-call | flops 1342177280 | bytes 7340032 | tf_op jit(solution)/shard_map/weights/pallas_call | solution.py:292
  31.9 3.3 %collective-permute-start.22 = (bf16[128,640]{1,0:T(8,128)(2,1)S(1)}, bf16[128,640]{1,0:T(8,128)(2,1)S(1)}, u32[]{:S(2)}, u32[]{:S(2)}) collective-permute-start(bf16[128,640]{1,0:T(8,128)(2,1)S(1)} %collective-permute-done.20.refs_4_), channel_id=1, source_target_pairs={{0,28},{4,0},{8,4},{12,8},{16,12},{20,16},{24,20},{28,24},{1,29},{... | collective-permute-start | bytes 491528 | tf_op jit(solution)/shard_map/ppermute | solution.py:251
  35.2 2.3 %weights.10 = (bf16[640,256]{1,0:T(8,128)(2,1)S(1)}, bf16[4096,256]{1,0:T(8,128)(2,1)S(1)}) custom-call(s32[8]{0:T(128)S(1)} %get-tuple-element.125.win, bf16[4,256,1024]{2,1,0:T(8,128)(2,1)S(1)} %get-tuple-element.126.hot_ref, s32[32,128]{1,0:T(8,128)S(1)} %get-tuple-element.127.slot_ref, f32[128,128]{1,0:T(8,128)S(1)} %get-tuple-element.128.symt_ref, ...), custom_call_target="tpu_custom_call" | custom-call | flops 1342177280 | bytes 7340032 | tf_op jit(solution)/shard_map/weights/pallas_call | solution.py:292
  37.6 2.3 %weights.11.refs_10_.refs_4_ = bf16[640,256]{1,0:T(8,128)(2,1)S(1)} custom-call(s32[8]{0:T(128)S(1)} %get-tuple-element.125.win, bf16[4,256,1024]{2,1,0:T(8,128)(2,1)S(1)} %get-tuple-element.126.hot_ref, s32[32,128]{1,0:T(8,128)S(1)} %get-tuple-element.127.slot_ref, f32[128,128]{1,0:T(8,128)S(1)} %get-tuple-element.128.symt_ref, ...), custom_call_target="tpu_custom_call" | custom-call | flops 1342177280 | bytes 7340032 | tf_op jit(solution)/shard_map/weights/pallas_call | solution.py:292
  40.0 2.1 %early.2.early_ref = f32[8,128,128]{2,1,0:T(8,128)S(1)} custom-call(s32[1,100]{1,0:T(1,128)S(1)} %bitcast.11, bf16[128,640]{1,0:T(8,128)(2,1)S(1)} %constant_dynamic-update-slice_fusion.4.refs_0_, bf16[128,640]{1,0:T(8,128)(2,1)S(1)} %collective-permute-done.17.refs_1_, bf16[128,640]{1,0:T(8,128)(2,1)S(1)} %collective-permute-done.18.refs_2_, ...), custom_call_target="tpu_custom_call" | custom-call | flops 1174405120 | bytes 4194304 | tf_op jit(solution)/shard_map/early/pallas_call | solution.py:320
  42.2 2.0 %collective-permute-done.23.refs_0_ = bf16[128,640]{1,0:T(8,128)(2,1)S(1)} collective-permute-done((bf16[128,640]{1,0:T(8,128)(2,1)S(1)}, bf16[128,640]{1,0:T(8,128)(2,1)S(1)}, u32[]{:S(2)}, u32[]{:S(2)}) %collective-permute-start.23) | collective-permute-done | bytes 163872 | tf_op jit(solution)/shard_map/ppermute | solution.py:251
  44.2 0.5 product.2
  44.8 1.5 %collective-permute-done.24.got_ref = f32[4,136,128]{2,1,0:T(8,128)S(1)} collective-permute-done((f32[4,136,128]{2,1,0:T(8,128)S(1)}, f32[4,136,128]{2,1,0:T(8,128)S(1)}, u32[]{:S(2)}, u32[]{:S(2)}) %collective-permute-start.24) | collective-permute-done | bytes 278560 | tf_op jit(solution)/shard_map/ppermute | solution.py:251
  46.4 1.3 %collective-permute-start.25 = (f32[136,128]{1,0:T(8,128)S(1)}, f32[136,128]{1,0:T(8,128)S(1)}, u32[]{:S(2)}, u32[]{:S(2)}) collective-permute-start(f32[136,128]{1,0:T(8,128)S(1)} %get-tuple-element.139), channel_id=1, source_target_pairs={{0,128},{64,192},{128,0},{192,64},{1,129},{65,193},{129,1},{193,65... | collective-permute-start | bytes 208904 | tf_op jit(solution)/shard_map/ppermute | solution.py:251
  47.7 2.2 %collective-permute-start.26 = (f32[136,128]{1,0:T(8,128)S(1)}, f32[136,128]{1,0:T(8,128)S(1)}, u32[]{:S(2)}, u32[]{:S(2)}) collective-permute-start(f32[136,128]{1,0:T(8,128)S(1)} %get-tuple-element.140), channel_id=1, source_target_pairs={{0,64},{64,128},{128,192},{192,0},{1,65},{65,129},{129,193},{193,1... | collective-permute-start | bytes 208904 | tf_op jit(solution)/shard_map/ppermute | solution.py:251
  49.9 2.5 %collective-permute-done.25.refs_1_ = f32[136,128]{1,0:T(8,128)S(1)} collective-permute-done((f32[136,128]{1,0:T(8,128)S(1)}, f32[136,128]{1,0:T(8,128)S(1)}, u32[]{:S(2)}, u32[]{:S(2)}) %collective-permute-start.25) | collective-permute-done | bytes 69664 | tf_op jit(solution)/shard_map/ppermute | solution.py:251
  52.4 3.0 %collective-permute-done.27.refs_3_ = f32[136,128]{1,0:T(8,128)S(1)} collective-permute-done((f32[136,128]{1,0:T(8,128)S(1)}, f32[136,128]{1,0:T(8,128)S(1)}, u32[]{:S(2)}, u32[]{:S(2)}) %collective-permute-start.27) | collective-permute-done | bytes 69664 | tf_op jit(solution)/shard_map/ppermute | solution.py:251
  55.4 1.0 %finish.2 = (bf16[128,1024]{1,0:T(8,128)(2,1)}, f32[128,128]{1,0:T(8,128)S(1)}, s32[1]{0:T(128)}) custom-call(s32[1,100]{1,0:T(1,128)S(1)} %bitcast.13, f32[136,128]{1,0:T(8,128)S(1)} %get-tuple-element.138.refs_0_, f32[136,128]{1,0:T(8,128)S(1)} %collective-permute-done.25.refs_1_, f32[136,128]{1,0:T(8,128)S(1)} %collective-permute-done.26.refs_2_, ...), custom_call_target="tpu_custom_call" | custom-call | tf_op jit(solution)/shard_map/finish/pallas_call | solution.py:355
  (26 shorter events, 0.5 us)
Async XLA Ops:
  4.7 5.7 %collective-permute-start.14 = (bf16[32,640]{1,0:T(8,128)(2,1)S(1)}, bf16[32,640]{1,0:T(8,128)(2,1)S(1)}, u32[]{:S(2)}, u32[]{:S(2)}) collective-permute-start(bf16[32,640]{1,0:T(8,128)(2,1)S(1)} %get-tuple-element.124), channel_id=1, source_target_pairs={{0,2},{1,3},{2,0},{3,1},{4,6},{5,7},{6,4},{7,5},{8,10},{9,11},{10,... | collective-permute-start | bytes 122888 | tf_op jit(solution)/shard_map/ppermute | solution.py:251
  6.2 4.2 %collective-permute-start.15 = (bf16[32,640]{1,0:T(8,128)(2,1)S(1)}, bf16[32,640]{1,0:T(8,128)(2,1)S(1)}, u32[]{:S(2)}, u32[]{:S(2)}) collective-permute-start(bf16[32,640]{1,0:T(8,128)(2,1)S(1)} %get-tuple-element.124), channel_id=1, source_target_pairs={{0,1},{1,2},{2,3},{3,0},{4,5},{5,6},{6,7},{7,4},{8,9},{9,10},{10,1... | collective-permute-start | bytes 122888 | tf_op jit(solution)/shard_map/ppermute | solution.py:251
  8.3 5.2 %collective-permute-start.16 = (bf16[32,640]{1,0:T(8,128)(2,1)S(1)}, bf16[32,640]{1,0:T(8,128)(2,1)S(1)}, u32[]{:S(2)}, u32[]{:S(2)}) collective-permute-start(bf16[32,640]{1,0:T(8,128)(2,1)S(1)} %get-tuple-element.124), channel_id=1, source_target_pairs={{0,3},{1,0},{2,1},{3,2},{4,7},{5,4},{6,5},{7,6},{8,11},{9,8},{10,9... | collective-permute-start | bytes 122888 | tf_op jit(solution)/shard_map/ppermute | solution.py:251
  13.5 9.1 %collective-permute-start.17 = (bf16[128,640]{1,0:T(8,128)(2,1)S(1)}, bf16[128,640]{1,0:T(8,128)(2,1)S(1)}, u32[]{:S(2)}, u32[]{:S(2)}) collective-permute-start(bf16[128,640]{1,0:T(8,128)(2,1)S(1)} %constant_dynamic-update-slice_fusion.4.refs_0_), channel_id=1, source_target_pairs={{0,4},{4,8},{8,12},{12,16},{16,20},{20,24},{24,28},{28,0},{1,5},{5... | collective-permute-start | bytes 491528 | tf_op jit(solution)/shard_map/ppermute | solution.py:251
  15.4 7.2 %collective-permute-start.18 = (bf16[128,640]{1,0:T(8,128)(2,1)S(1)}, bf16[128,640]{1,0:T(8,128)(2,1)S(1)}, u32[]{:S(2)}, u32[]{:S(2)}) collective-permute-start(bf16[128,640]{1,0:T(8,128)(2,1)S(1)} %constant_dynamic-update-slice_fusion.4.refs_0_), channel_id=1, source_target_pairs={{0,28},{4,0},{8,4},{12,8},{16,12},{20,16},{24,20},{28,24},{1,29},{... | collective-permute-start | bytes 491528 | tf_op jit(solution)/shard_map/ppermute | solution.py:251
  22.6 6.6 %collective-permute-start.19 = (bf16[128,640]{1,0:T(8,128)(2,1)S(1)}, bf16[128,640]{1,0:T(8,128)(2,1)S(1)}, u32[]{:S(2)}, u32[]{:S(2)}) collective-permute-start(bf16[128,640]{1,0:T(8,128)(2,1)S(1)} %collective-permute-done.17.refs_1_), channel_id=1, source_target_pairs={{0,4},{4,8},{8,12},{12,16},{16,20},{20,24},{24,28},{28,0},{1,5},{5... | collective-permute-start | bytes 491528 | tf_op jit(solution)/shard_map/ppermute | solution.py:251
  22.7 9.2 %collective-permute-start.20 = (bf16[128,640]{1,0:T(8,128)(2,1)S(1)}, bf16[128,640]{1,0:T(8,128)(2,1)S(1)}, u32[]{:S(2)}, u32[]{:S(2)}) collective-permute-start(bf16[128,640]{1,0:T(8,128)(2,1)S(1)} %collective-permute-done.18.refs_2_), channel_id=1, source_target_pairs={{0,28},{4,0},{8,4},{12,8},{16,12},{20,16},{24,20},{28,24},{1,29},{... | collective-permute-start | bytes 491528 | tf_op jit(solution)/shard_map/ppermute | solution.py:251
  29.3 8.3 %collective-permute-start.21 = (bf16[128,640]{1,0:T(8,128)(2,1)S(1)}, bf16[128,640]{1,0:T(8,128)(2,1)S(1)}, u32[]{:S(2)}, u32[]{:S(2)}) collective-permute-start(bf16[128,640]{1,0:T(8,128)(2,1)S(1)} %collective-permute-done.19.refs_3_), channel_id=1, source_target_pairs={{0,4},{4,8},{8,12},{12,16},{16,20},{20,24},{24,28},{28,0},{1,5},{5... | collective-permute-start | bytes 491528 | tf_op jit(solution)/shard_map/ppermute | solution.py:251
  31.9 8.1 %collective-permute-start.22 = (bf16[128,640]{1,0:T(8,128)(2,1)S(1)}, bf16[128,640]{1,0:T(8,128)(2,1)S(1)}, u32[]{:S(2)}, u32[]{:S(2)}) collective-permute-start(bf16[128,640]{1,0:T(8,128)(2,1)S(1)} %collective-permute-done.20.refs_4_), channel_id=1, source_target_pairs={{0,28},{4,0},{8,4},{12,8},{16,12},{20,16},{24,20},{28,24},{1,29},{... | collective-permute-start | bytes 491528 | tf_op jit(solution)/shard_map/ppermute | solution.py:251
  37.5 6.6 %collective-permute-start.23 = (bf16[128,640]{1,0:T(8,128)(2,1)S(1)}, bf16[128,640]{1,0:T(8,128)(2,1)S(1)}, u32[]{:S(2)}, u32[]{:S(2)}) collective-permute-start(bf16[128,640]{1,0:T(8,128)(2,1)S(1)} %collective-permute-done.21.refs_5_), channel_id=1, source_target_pairs={{0,4},{4,8},{8,12},{12,16},{16,20},{20,24},{24,28},{28,0},{1,5},{5... | collective-permute-start | bytes 491528 | tf_op jit(solution)/shard_map/ppermute | solution.py:251
  37.6 2.3 %copy-start.3 = (s32[100]{0:T(128)S(1)}, s32[100]{0:T(128)}, u32[]{:S(2)}) copy-start(s32[100]{0:T(128)} %param.12) | copy-start | bytes 1204
  42.1 14.8 %copy-start = (bf16[32,4096]{1,0:T(8,128)(2,1)S(1)}, bf16[32,4096]{1,0:T(8,128)(2,1)}, u32[]{:S(2)}) copy-start(bf16[32,4096]{1,0:T(8,128)(2,1)} %amp_ref.1) | copy-start | bytes 786436
  42.2 14.8 %copy-start.1 = (s32[2,4096]{1,0:T(2,128)S(1)}, s32[2,4096]{1,0:T(2,128)}, u32[]{:S(2)}) copy-start(s32[2,4096]{1,0:T(2,128)} %cd_ref.1) | copy-start | bytes 98308
  42.2 14.8 %copy-start.2 = (s32[1200]{0:T(1024)S(1)}, s32[1200]{0:T(1024)}, u32[]{:S(2)}) copy-start(s32[1200]{0:T(1024)} %vir_ref.1) | copy-start | bytes 14404
  44.7 1.6 %collective-permute-start.24 = (f32[4,136,128]{2,1,0:T(8,128)S(1)}, f32[4,136,128]{2,1,0:T(8,128)S(1)}, u32[]{:S(2)}, u32[]{:S(2)}) collective-permute-start(f32[4,136,128]{2,1,0:T(8,128)S(1)} %get-tuple-element.137), channel_id=1, source_target_pairs={{0,32},{32,0},{1,33},{33,1},{2,34},{34,2},{3,35},{35,3},{4,36},{36... | collective-permute-start | bytes 835592 | tf_op jit(solution)/shard_map/ppermute | solution.py:251
  46.4 6.0 %collective-permute-start.25 = (f32[136,128]{1,0:T(8,128)S(1)}, f32[136,128]{1,0:T(8,128)S(1)}, u32[]{:S(2)}, u32[]{:S(2)}) collective-permute-start(f32[136,128]{1,0:T(8,128)S(1)} %get-tuple-element.139), channel_id=1, source_target_pairs={{0,128},{64,192},{128,0},{192,64},{1,129},{65,193},{129,1},{193,65... | collective-permute-start | bytes 208904 | tf_op jit(solution)/shard_map/ppermute | solution.py:251
  47.7 4.7 %collective-permute-start.26 = (f32[136,128]{1,0:T(8,128)S(1)}, f32[136,128]{1,0:T(8,128)S(1)}, u32[]{:S(2)}, u32[]{:S(2)}) collective-permute-start(f32[136,128]{1,0:T(8,128)S(1)} %get-tuple-element.140), channel_id=1, source_target_pairs={{0,64},{64,128},{128,192},{192,0},{1,65},{65,129},{129,193},{193,1... | collective-permute-start | bytes 208904 | tf_op jit(solution)/shard_map/ppermute | solution.py:251
  49.9 5.5 %collective-permute-start.27 = (f32[136,128]{1,0:T(8,128)S(1)}, f32[136,128]{1,0:T(8,128)S(1)}, u32[]{:S(2)}, u32[]{:S(2)}) collective-permute-start(f32[136,128]{1,0:T(8,128)S(1)} %get-tuple-element.141), channel_id=1, source_target_pairs={{0,192},{64,0},{128,64},{192,128},{1,193},{65,1},{129,65},{193,129... | collective-permute-start | bytes 208904 | tf_op jit(solution)/shard_map/ppermute | solution.py:251
where the time goes:
time: 57.5 us; the launch traced here: 57.4 us
  starting transfers between devices  19.8 us (34%)
  waiting for transfers between devices  18.4 us (32%)
  Pallas kernels  17.9 us (31%)
  between operations  0.92 us (2%)
    ppermute x14, starting transfers between devices, shift(): return lax.ppermute(a, axis, [(i, (i + k) % size) for i in range(size)])  19.8 us
    ppermute x14, waiting for transfers between devices, shift(): return lax.ppermute(a, axis, [(i, (i + k) % size) for i in range(size)])  18.4 us
    pallas_call x4, Pallas kernels, round_body(): pl.pallas_call(functools.partial(weights_kernel, k, more), out_shape=out,...  9.56 us
    pallas_call x1, Pallas kernels, round_body(): pl.pallas_call(functools.partial(pack_kernel, n_occ, n_vir), out_shape=(s...  4.67 us
    pallas_call x1, Pallas kernels, round_body(): pl.pallas_call(functools.partial(early_kernel, n_occ, places[:-1]), out_s...  2.14 us
  transfers between devices with their start and end apart: 14, of which 8 were waited for; matrix products, arithmetic and copies ran while one was open for 0% of the time, Pallas kernels for 20%

commit v1 on v0

--- a/solution.py
+++ b/solution.py
@@ -37,10 +37,9 @@
 
 
 def pack_kernel(
-    n_occ, n_vir, start, occ_ref, vir_ref, cd_ref, amp_ref, w_ref,
-    t_ref, hot_ref, slot_ref, symt_ref, cnt_ref, win_ref, next_ref, occ_s, vir_s, idx_s, acc, kept, sem
+    n_occ, n_vir, start, occ_ref, vir_ref, cd_ref, amp_ref,
+    t_ref, hot_ref, slot_ref, symt_ref, cnt_ref, win_ref, occ_s, vir_s, idx_s, acc, kept
 ):
-    load = quarter(w_ref, next_ref, 0, sem)
     rows, pairs = amp_ref.shape
     chunks = pairs // LANES
     occ_s[...] = jnp.zeros_like(occ_s)
@@ -119,7 +118,6 @@
             place(kept[:, c * CHUNK : (c + 1) * CHUNK], one_hot(lines(slot_ref[...], c, per), at), at)
 
     t_ref[...] = acc[:, :SLOTS].astype(BF16)
-    load.wait()
 
 
 def lines(a, c, per):
@@ -134,6 +132,17 @@
     copy = pltpu.make_async_copy(w_ref.at[:, part * WIDTH : (part + 1) * WIDTH], into, sem)
     copy.start()
     return copy
+
+
+def first_weights_kernel(win, hot_ref, slot_ref, symt_ref, w_ref, out_ref, next_ref, kept, acc, raw, sems, sem):
+    copies = []
+    for c in range(w_ref.shape[0] // CHUNK):
+        rows = slice(c * CHUNK, (c + 1) * CHUNK)
+        copies.append(pltpu.make_async_copy(w_ref.at[rows, :WIDTH], raw.at[rows], sems.at[c]))
+        copies[-1].start()
+    load = quarter(w_ref, next_ref, 1, sem)
+    pack_weights(0, win, hot_ref, slot_ref, symt_ref, raw, out_ref, kept, acc, copies)
+    load.wait()
 
 
 def weights_kernel(part, more, win, hot_ref, slot_ref, symt_ref, ready_ref, *refs):
@@ -142,10 +151,18 @@
         load = quarter(w_ref, next_ref, part + 1, sem)
     else:
         out_ref, kept, acc = refs
+    pack_weights(part, win, hot_ref, slot_ref, symt_ref, ready_ref, out_ref, kept, acc)
+    if more:
+        load.wait()
+
+
+def pack_weights(part, win, hot_ref, slot_ref, symt_ref, ready_ref, out_ref, kept, acc, copies=None):
     width = out_ref.shape[1]
     per = CHUNK // LANES
     acc[...] = jnp.zeros_like(acc)
     for c in range(ready_ref.shape[0] // CHUNK):
+        if copies:
+            copies[c].wait()
         for m in range(per):
             sym = jnp.broadcast_to(symt_ref[:, c * per + m : c * per + m + 1], (LANES, LANES)).astype(BF16)
             rows = slice(c * CHUNK + m * LANES, c * CHUNK + (m + 1) * LANES)
@@ -164,20 +181,19 @@
             acc[pl.ds(at, WINDOW), :] += jnp.dot(one, kept[...], preferred_element_type=F32)
 
     out_ref[...] = acc[:SLOTS].astype(BF16)
-    if more:
-        load.wait()
 
 
 def multiply(n_occ, places, occ_ref, blocks, weights, out, occ_s):
     z, x = lax.axis_index("z"), lax.axis_index("x")
+    sign = 2 * (z % 2) - 1
     occ_s[...] = jnp.zeros_like(occ_s)
     occ_s[:, :n_occ] = occ_ref[...]
     for ref, (dz, order) in zip(blocks, places):
         height = ref.shape[0]
-        owner = (z + dz) % 8
+        owner = (z + dz * sign + 8) % 8
         total = jnp.zeros((height, LANES), F32)
         piece = height // len(order)
-        starts = [owner * height + (x + dx) % 4 * piece for dx in order]
+        starts = [owner * height + jnp.bitwise_xor(x, dx) * piece for dx in order]
         cls = jnp.concatenate([row_classes(occ_s[...], at, piece, n_occ) for at in starts], axis=0)
         for p, w in enumerate(weights):
             part = jnp.dot(ref[...], w[...], preferred_element_type=F32)
@@ -185,7 +201,7 @@
                 g = p * (w.shape[1] // LANES) + q
                 total = total + jnp.where(cls == g, part[:, q * LANES : (q + 1) * LANES], 0.0)
         for j, dx in enumerate(order):
-            at = pl.ds(pl.multiple_of((x + dx) % 4 * piece, piece), piece)
+            at = pl.ds(pl.multiple_of(jnp.bitwise_xor(x, dx) * piece, piece), piece)
             out[owner, at] = total[j * piece : (j + 1) * piece]
 
 
@@ -200,7 +216,7 @@
     keep_ref, send_ref, sums_s, occ_s = refs[-4:]
     multiply(n_occ, places, occ_ref, refs[:n], refs[n:-4], sums_s, occ_s)
     core, z = lax.axis_index("core"), lax.axis_index("z")
-    late = (z + places[0][0]) % 8
+    late = (z + 4) % 8
     for ref, odd in ((keep_ref, core), (send_ref, 1 - core)):
         for k in range(4):
             owner = 2 * k + odd
@@ -216,15 +232,15 @@
             ref[k, 128:] = cnt_ref[...]
 
 
-def fold_kernel(keep_ref, got_ref, *outs):
+def fold_kernel(order, keep_ref, got_ref, *outs):
     y = lax.axis_index("y")
-    for k, out in enumerate(outs):
-        at = (y + k) % 4
+    for k, out in zip(order, outs):
+        at = jnp.bitwise_xor(y, k)
         out[:128] = keep_ref[at, :128] + got_ref[at, :128]
         out[128:] = jnp.maximum(keep_ref[at, 128:], got_ref[at, 128:])
 
 
-def finish_kernel(n_occ, occ_ref, prev_ref, a, b, c, d, out_ref, sum_ref, most_ref, occ_s):
+def finish_kernel(n_occ, occ_ref, prev_ref, a, b, c, d, out_ref, sum_ref, most_ref, more_ref, occ_s):
     first = (lax.axis_index("y") * 2 + lax.axis_index("core")) * 128
     occ_s[...] = jnp.zeros_like(occ_s)
     occ_s[:, :n_occ] = occ_ref[...]
@@ -235,6 +251,7 @@
     sum_ref[...] = total
     most = jnp.maximum(jnp.maximum(a[128:], b[128:]), jnp.maximum(c[128:], d[128:]))
     most_ref[0] = jnp.max(most).astype(I32)
+    more_ref[0] = (most_ref[0] > SLOTS).astype(I32)
     for g in range(CLASSES):
         out_ref[:, g * LANES : (g + 1) * LANES] = jnp.where(cls == g, total, 0.0).astype(BF16)
 
@@ -247,8 +264,17 @@
     return pl.CostEstimate(flops=flops, bytes_accessed=nbytes, transcendentals=0)
 
 
-def shift(a, axis, size, k):
-    return lax.ppermute(a, axis, [(i, (i + k) % size) for i in range(size)])
+def swap(a, axis, partner):
+    pairs = [(i, partner(i)) for i in range(lax.axis_size(axis))]
+    return lax.ppermute(a, axis, pairs)
+
+
+def across(i):
+    return (i + 1 if i % 2 else i + 7) % 8
+
+
+def beside(i):
+    return i ^ 1
 
 
 def round_body(start, prev, amplitudes, integrals, occ_irrep, vir_irrep, cd_list):
@@ -257,7 +283,7 @@
     cols = integrals.shape[1]
     sds = jax.ShapeDtypeStruct
     occ = occ_irrep.reshape(1, n_occ)
-    packed, hot, slot, symt, most, win, ready = pl.pallas_call(
+    packed, hot, slot, symt, most, win = pl.pallas_call(
         functools.partial(pack_kernel, n_occ, n_vir),
         out_shape=(
             sds((rows, SLOTS), BF16),
@@ -266,55 +292,59 @@
             sds((LANES, LANES), F32),
             sds((8, LANES), F32),
             sds((2 * pairs // CHUNK,), I32),
-            pltpu.VMEM((pairs, WIDTH), BF16),
         ),
-        in_specs=[SMEM, VMEM, VMEM, VMEM, VMEM, ANY],
-        out_specs=(VMEM,) * 5 + (SMEM, VMEM),
+        in_specs=[SMEM, VMEM, VMEM, VMEM, VMEM],
+        out_specs=(VMEM,) * 5 + (SMEM,),
         scratch_shapes=[
             pltpu.VMEM((1, LANES), I32),
             pltpu.VMEM((1, 10 * LANES), I32),
             pltpu.VMEM((2 * pairs // LANES, LANES), I32),
             pltpu.VMEM((rows, SLOTS + 3 * LANES), F32),
             pltpu.VMEM((rows, pairs), BF16),
-            pltpu.SemaphoreType.DMA,
         ],
         compiler_params=params(8),
         cost_estimate=cost(2 * rows * pairs * SLOTS, 6 << 20),
         name="pack",
-    )(start, occ, vir_irrep, cd_list, amplitudes, integrals)
+    )(start, occ, vir_irrep, cd_list, amplitudes)
 
     parts = []
     count = cols // WIDTH
+    quarter_of = pltpu.VMEM((pairs, WIDTH), BF16)
     for k in range(count):
         more = k + 1 < count
-        out = (sds((SLOTS, WIDTH), BF16),) + more * (pltpu.VMEM((pairs, WIDTH), BF16),)
+        out = (sds((SLOTS, WIDTH), BF16),) + more * (quarter_of,)
         scratch = [pltpu.VMEM((CHUNK, WIDTH), BF16), pltpu.VMEM((SLOTS + WINDOW, WIDTH), F32)]
+        if k == 0:
+            kernel, given, specs = first_weights_kernel, (integrals,), [ANY]
+            scratch += [quarter_of, pltpu.SemaphoreType.DMA((pairs // CHUNK,))]
+        else:
+            kernel, given, specs = functools.partial(weights_kernel, k, more), (ready, integrals), [VMEM, ANY]
+        if not more:
+            given, specs = given[:1], specs[:1]
         part, *ready = pl.pallas_call(
-            functools.partial(weights_kernel, k, more),
+            kernel,
             out_shape=out,
-            in_specs=[SMEM, VMEM, VMEM, VMEM, VMEM] + more * [ANY],
+            in_specs=[SMEM, VMEM, VMEM, VMEM] + specs,
             out_specs=(VMEM,) * len(out),
             scratch_shapes=scratch + more * [pltpu.SemaphoreType.DMA],
             compiler_params=params(16),
             cost_estimate=cost(2 * WIDTH * pairs * SLOTS, 7 << 20),
             name="weights",
-        )(win, hot, slot, symt, ready, *(more * (integrals,)))
+        )(win, hot, slot, symt, *given)
         parts.append(part)
         ready = ready[0] if more else None
 
-    near = [packed] + [shift(packed, "x", 4, k) for k in (2, 1, 3)]
     order = (0, 2, 3, 1)
+    near = [packed] + [swap(packed, "x", lambda i, m=m: i ^ m) for m in order[1:]]
     mine = jnp.concatenate(near, axis=0)
     blocks, places = [mine], [(0, order)]
-    up = down = mine
-    for k in range(1, 5):
-        up = shift(up, "z", 8, 1)
-        blocks.append(up)
-        places.append((8 - k, order))
-        if k < 4:
-            down = shift(down, "z", 8, 7)
-            blocks.append(down)
-            places.append((k, order))
+    far, close = mine, mine
+    for k in range(1, 4):
+        far, close = swap(close, "z", across), swap(far, "z", beside)
+        blocks += [far, close]
+        places += [(k, order), (-k, order)]
+    blocks.append(swap(far, "z", beside))
+    places.append((4, order))
 
     sums = sds((8, 128, LANES), F32)
     early = pl.pallas_call(
@@ -338,25 +368,25 @@
         name="product",
     )(occ, most, early, blocks[-1], *parts)
 
-    got = shift(send, "core", 2, 1)
+    got = swap(send, "core", beside)
     folded = pl.pallas_call(
-        fold_kernel,
+        functools.partial(fold_kernel, order),
         out_shape=(sds((136, LANES), F32),) * 4,
         in_specs=[VMEM] * 2,
         out_specs=(VMEM,) * 4,
         compiler_params=params(8),
         name="fold",
     )(keep, got)
-    arrived = [folded[0]] + [shift(folded[k], "y", 4, k) for k in (2, 1, 3)]
+    arrived = [folded[0]] + [swap(f, "y", lambda i, m=m: i ^ m) for m, f in zip(order[1:], folded[1:])]
     kernel = functools.partial(finish_kernel, n_occ)
     if prev is None:
         kernel = lambda occ_ref, *refs: finish_kernel(n_occ, occ_ref, None, *refs)
     extra = () if prev is None else (prev,)
     return pl.pallas_call(
         kernel,
-        out_shape=(sds((128, cols), BF16), sds((128, LANES), F32), sds((1,), I32)),
+        out_shape=(sds((128, cols), BF16), sds((128, LANES), F32), sds((1,), I32), sds((1,), I32)),
         in_specs=[VMEM] * (5 + len(extra)),
-        out_specs=(VMEM, VMEM, SMEM),
+        out_specs=(VMEM, VMEM, SMEM, SMEM),
         scratch_shapes=[pltpu.VMEM((1, LANES), I32)],
         compiler_params=params(8),
         name="finish",
@@ -365,17 +395,17 @@
 
 def local(amplitudes, integrals, occ_irrep, vir_irrep, cd_list, ab_list):
     args = (amplitudes, integrals, occ_irrep, vir_irrep, cd_list)
-    out, total, most = round_body(jnp.zeros((1,), I32), None, *args)
+    out, total, most, more_rounds = round_body(jnp.zeros((1,), I32), None, *args)
 
     def more(out, total, most):
         def body(state):
             k, _, total = state
-            out, total, _ = round_body((k * SLOTS).reshape(1), total, *args)
+            out, total, _, _ = round_body((k * SLOTS).reshape(1), total, *args)
             return k + 1, out, total
 
         return lax.while_loop(lambda s: s[0] * SLOTS < most[0], body, (jnp.int32(1), out, total))[1]
 
-    return lax.cond(most[0] > SLOTS, more, lambda out, total, most: out, out, total, most)
+    return lax.switch(more_rounds[0], (lambda out, total, most: out, more), out, total, most)
 
 
 def solution(mesh):

time: 57.5 us -> 56 us (0.974)
  the two profiles are of different devices: /device:TPU:30 before, /device:TPU:1 now
where the time goes in v1:
time: 56 us; the launch traced here: 55.9 us
  starting transfers between devices  24.1 us (43%)
  Pallas kernels  17.8 us (32%)
  waiting for transfers between devices  12.7 us (23%)
  between operations  0.99 us (2%)
    ppermute x14, starting transfers between devices, swap(): return lax.ppermute(a, axis, pairs)  24.1 us
    ppermute x14, waiting for transfers between devices, swap(): return lax.ppermute(a, axis, pairs)  12.7 us
    pallas_call x4, Pallas kernels, round_body(): pl.pallas_call(kernel, out_shape=out, in_specs=[SMEM, VMEM, VMEM, VMEM] +...  10.6 us
    pallas_call x1, Pallas kernels, round_body(): pl.pallas_call(functools.partial(pack_kernel, n_occ, n_vir), out_shape=(s...  3.38 us
    pallas_call x1, Pallas kernels, round_body(): pl.pallas_call(functools.partial(early_kernel, n_occ, places[:-1]), out_s...  2.19 us
  transfers between devices with their start and end apart: 14, of which 7 were waited for; matrix products, arithmetic and copies ran while one was open for 0% of the time, Pallas kernels for 23%

profile of v1, /device:TPU:1, one launch (start us, length us, event | category | flops | bytes accessed | tf_op | source)
XLA Modules:
  0.0 55.9 jit_solution(11082026138992917156)
XLA Ops:
  0.0 3.4 %pack.2 = (bf16[32,640]{1,0:T(8,128)(2,1)S(1)}, bf16[4,256,1024]{2,1,0:T(8,128)(2,1)S(1)}, s32[32,128]{1,0:T(8,128)S(1)}, f32[128,128]{1,0:T(8,128)S(1)}, f32[8,128]{1,0:T(8,128)S(1)}, /*index=5*/s32[8]{0:T(128)S(1)}) custom-call(s32[1]{0:T(128)} %constant.4.clone.1.start, s32[1,100]{1,0:T(1,128)} %bitcast.10, s32[1200]{0:T(1024)} %vir_ref.1, ...), custom_call_target="tpu_custom_call" | custom-call | flops 167772160 | bytes 6291456 | tf_op jit(solution)/shard_map/pack/pallas_call | solution.py:286
  3.4 3.7 %collective-permute-start.14 = (bf16[32,640]{1,0:T(8,128)(2,1)S(1)}, bf16[32,640]{1,0:T(8,128)(2,1)S(1)}, u32[]{:S(2)}, u32[]{:S(2)}) collective-permute-start(bf16[32,640]{1,0:T(8,128)(2,1)S(1)} %get-tuple-element.123), channel_id=1, source_target_pairs={{0,2},{1,3},{2,0},{3,1},{4,6},{5,7},{6,4},{7,5},{8,10},{9,11},{10,... | collective-permute-start | bytes 122888 | tf_op jit(solution)/shard_map/ppermute | solution.py:269
  7.0 0.9 %collective-permute-start.15 = (bf16[32,640]{1,0:T(8,128)(2,1)S(1)}, bf16[32,640]{1,0:T(8,128)(2,1)S(1)}, u32[]{:S(2)}, u32[]{:S(2)}) collective-permute-start(bf16[32,640]{1,0:T(8,128)(2,1)S(1)} %get-tuple-element.123), channel_id=1, source_target_pairs={{0,3},{1,2},{2,1},{3,0},{4,7},{5,6},{6,5},{7,4},{8,11},{9,10},{10,... | collective-permute-start | bytes 122888 | tf_op jit(solution)/shard_map/ppermute | solution.py:269
  7.9 0.5 collective-permute-done.14
  8.4 3.0 %collective-permute-done.15 = bf16[32,640]{1,0:T(8,128)(2,1)S(1)} collective-permute-done((bf16[32,640]{1,0:T(8,128)(2,1)S(1)}, bf16[32,640]{1,0:T(8,128)(2,1)S(1)}, u32[]{:S(2)}, u32[]{:S(2)}) %collective-permute-start.15) | collective-permute-done | bytes 40992 | tf_op jit(solution)/shard_map/ppermute | solution.py:269
  11.4 5.4 %collective-permute-start.17 = (bf16[128,640]{1,0:T(8,128)(2,1)S(1)}, bf16[128,640]{1,0:T(8,128)(2,1)S(1)}, u32[]{:S(2)}, u32[]{:S(2)}) collective-permute-start(bf16[128,640]{1,0:T(8,128)(2,1)S(1)} %constant_dynamic-update-slice_fusion.4.refs_0_), channel_id=1, source_target_pairs={{0,28},{4,8},{8,4},{12,16},{16,12},{20,24},{24,20},{28,0},{1,29},{... | collective-permute-start | bytes 491528 | tf_op jit(solution)/shard_map/ppermute | solution.py:269
  16.8 2.7 %collective-permute-done.17.refs_1_ = bf16[128,640]{1,0:T(8,128)(2,1)S(1)} collective-permute-done((bf16[128,640]{1,0:T(8,128)(2,1)S(1)}, bf16[128,640]{1,0:T(8,128)(2,1)S(1)}, u32[]{:S(2)}, u32[]{:S(2)}) %collective-permute-start.17) | collective-permute-done | bytes 163872 | tf_op jit(solution)/shard_map/ppermute | solution.py:269
  19.5 1.8 %collective-permute-done.18.refs_2_ = bf16[128,640]{1,0:T(8,128)(2,1)S(1)} collective-permute-done((bf16[128,640]{1,0:T(8,128)(2,1)S(1)}, bf16[128,640]{1,0:T(8,128)(2,1)S(1)}, u32[]{:S(2)}, u32[]{:S(2)}) %collective-permute-start.18) | collective-permute-done | bytes 163872 | tf_op jit(solution)/shard_map/ppermute | solution.py:269
  21.3 0.9 %collective-permute-start.19 = (bf16[128,640]{1,0:T(8,128)(2,1)S(1)}, bf16[128,640]{1,0:T(8,128)(2,1)S(1)}, u32[]{:S(2)}, u32[]{:S(2)}) collective-permute-start(bf16[128,640]{1,0:T(8,128)(2,1)S(1)} %collective-permute-done.18.refs_2_), channel_id=1, source_target_pairs={{0,28},{4,8},{8,4},{12,16},{16,12},{20,24},{24,20},{28,0},{1,29},{... | collective-permute-start | bytes 491528 | tf_op jit(solution)/shard_map/ppermute | solution.py:269
  22.2 3.4 %weights.8 = (bf16[640,256]{1,0:T(8,128)(2,1)S(1)}, bf16[4096,256]{1,0:T(8,128)(2,1)S(1)}) custom-call(s32[8]{0:T(128)S(1)} %get-tuple-element.124.win, bf16[4,256,1024]{2,1,0:T(8,128)(2,1)S(1)} %get-tuple-element.125.hot_ref, s32[32,128]{1,0:T(8,128)S(1)} %get-tuple-element.126.slot_ref, f32[128,128]{1,0:T(8,128)S(1)} %get-tuple-element.127.symt_ref, ...), custom_call_target="tpu_custom_call" | custom-call | flops 1342177280 | bytes 7340032 | tf_op jit(solution)/shard_map/weights/pallas_call | solution.py:324
  25.6 1.8 %collective-permute-start.21 = (bf16[128,640]{1,0:T(8,128)(2,1)S(1)}, bf16[128,640]{1,0:T(8,128)(2,1)S(1)}, u32[]{:S(2)}, u32[]{:S(2)}) collective-permute-start(bf16[128,640]{1,0:T(8,128)(2,1)S(1)} %collective-permute-done.20.refs_4_), channel_id=1, source_target_pairs={{0,28},{4,8},{8,4},{12,16},{16,12},{20,24},{24,20},{28,0},{1,29},{... | collective-permute-start | bytes 491528 | tf_op jit(solution)/shard_map/ppermute | solution.py:269
  27.4 2.3 %weights.9 = (bf16[640,256]{1,0:T(8,128)(2,1)S(1)}, bf16[4096,256]{1,0:T(8,128)(2,1)S(1)}) custom-call(s32[8]{0:T(128)S(1)} %get-tuple-element.124.win, bf16[4,256,1024]{2,1,0:T(8,128)(2,1)S(1)} %get-tuple-element.125.hot_ref, s32[32,128]{1,0:T(8,128)S(1)} %get-tuple-element.126.slot_ref, f32[128,128]{1,0:T(8,128)S(1)} %get-tuple-element.127.symt_ref, ...), custom_call_target="tpu_custom_call" | custom-call | flops 1342177280 | bytes 7340032 | tf_op jit(solution)/shard_map/weights/pallas_call | solution.py:324
  29.9 2.6 %weights.10 = (bf16[640,256]{1,0:T(8,128)(2,1)S(1)}, bf16[4096,256]{1,0:T(8,128)(2,1)S(1)}) custom-call(s32[8]{0:T(128)S(1)} %get-tuple-element.124.win, bf16[4,256,1024]{2,1,0:T(8,128)(2,1)S(1)} %get-tuple-element.125.hot_ref, s32[32,128]{1,0:T(8,128)S(1)} %get-tuple-element.126.slot_ref, f32[128,128]{1,0:T(8,128)S(1)} %get-tuple-element.127.symt_ref, ...), custom_call_target="tpu_custom_call" | custom-call | flops 1342177280 | bytes 7340032 | tf_op jit(solution)/shard_map/weights/pallas_call | solution.py:324
  32.5 1.5 %collective-permute-start.23 = (bf16[128,640]{1,0:T(8,128)(2,1)S(1)}, bf16[128,640]{1,0:T(8,128)(2,1)S(1)}, u32[]{:S(2)}, u32[]{:S(2)}) collective-permute-start(bf16[128,640]{1,0:T(8,128)(2,1)S(1)} %collective-permute-done.21.refs_5_), channel_id=1, source_target_pairs={{0,4},{4,0},{8,12},{12,8},{16,20},{20,16},{24,28},{28,24},{1,5},{5... | collective-permute-start | bytes 491528 | tf_op jit(solution)/shard_map/ppermute | solution.py:269
  34.0 2.3 %weights.11.refs_10_.refs_4_ = bf16[640,256]{1,0:T(8,128)(2,1)S(1)} custom-call(s32[8]{0:T(128)S(1)} %get-tuple-element.124.win, bf16[4,256,1024]{2,1,0:T(8,128)(2,1)S(1)} %get-tuple-element.125.hot_ref, s32[32,128]{1,0:T(8,128)S(1)} %get-tuple-element.126.slot_ref, f32[128,128]{1,0:T(8,128)S(1)} %get-tuple-element.127.symt_ref, ...), custom_call_target="tpu_custom_call" | custom-call | flops 1342177280 | bytes 7340032 | tf_op jit(solution)/shard_map/weights/pallas_call | solution.py:324
  36.4 2.2 %early.2.early_ref = f32[8,128,128]{2,1,0:T(8,128)S(1)} custom-call(s32[1,100]{1,0:T(1,128)S(1)} %bitcast.11, bf16[128,640]{1,0:T(8,128)(2,1)S(1)} %constant_dynamic-update-slice_fusion.4.refs_0_, bf16[128,640]{1,0:T(8,128)(2,1)S(1)} %collective-permute-done.17.refs_1_, bf16[128,640]{1,0:T(8,128)(2,1)S(1)} %collective-permute-done.18.refs_2_, ...), custom_call_target="tpu_custom_call" | custom-call | flops 1174405120 | bytes 4194304 | tf_op jit(solution)/shard_map/early/pallas_call | solution.py:350
  38.6 0.5 product.2
  39.2 6.1 %collective-permute-start.24 = (f32[4,136,128]{2,1,0:T(8,128)S(1)}, f32[4,136,128]{2,1,0:T(8,128)S(1)}, u32[]{:S(2)}, u32[]{:S(2)}) collective-permute-start(f32[4,136,128]{2,1,0:T(8,128)S(1)} %get-tuple-element.135), channel_id=1, source_target_pairs={{0,32},{32,0},{1,33},{33,1},{2,34},{34,2},{3,35},{35,3},{4,36},{36... | collective-permute-start | bytes 835592 | tf_op jit(solution)/shard_map/ppermute | solution.py:269
  45.2 1.2 %collective-permute-done.24.got_ref = f32[4,136,128]{2,1,0:T(8,128)S(1)} collective-permute-done((f32[4,136,128]{2,1,0:T(8,128)S(1)}, f32[4,136,128]{2,1,0:T(8,128)S(1)}, u32[]{:S(2)}, u32[]{:S(2)}) %collective-permute-start.24) | collective-permute-done | bytes 278560 | tf_op jit(solution)/shard_map/ppermute | solution.py:269
  46.5 3.0 %collective-permute-start.25 = (f32[136,128]{1,0:T(8,128)S(1)}, f32[136,128]{1,0:T(8,128)S(1)}, u32[]{:S(2)}, u32[]{:S(2)}) collective-permute-start(f32[136,128]{1,0:T(8,128)S(1)} %get-tuple-element.137), channel_id=1, source_target_pairs={{0,128},{64,192},{128,0},{192,64},{1,129},{65,193},{129,1},{193,65... | collective-permute-start | bytes 208904 | tf_op jit(solution)/shard_map/ppermute | solution.py:269
  49.5 0.8 %collective-permute-start.26 = (f32[136,128]{1,0:T(8,128)S(1)}, f32[136,128]{1,0:T(8,128)S(1)}, u32[]{:S(2)}, u32[]{:S(2)}) collective-permute-start(f32[136,128]{1,0:T(8,128)S(1)} %get-tuple-element.138), channel_id=1, source_target_pairs={{0,192},{64,128},{128,64},{192,0},{1,193},{65,129},{129,65},{193,1... | collective-permute-start | bytes 208904 | tf_op jit(solution)/shard_map/ppermute | solution.py:269
  50.2 1.0 %collective-permute-done.25.refs_1_ = f32[136,128]{1,0:T(8,128)S(1)} collective-permute-done((f32[136,128]{1,0:T(8,128)S(1)}, f32[136,128]{1,0:T(8,128)S(1)}, u32[]{:S(2)}, u32[]{:S(2)}) %collective-permute-start.25) | collective-permute-done | bytes 69664 | tf_op jit(solution)/shard_map/ppermute | solution.py:269
  51.2 2.6 %collective-permute-done.26.refs_2_ = f32[136,128]{1,0:T(8,128)S(1)} collective-permute-done((f32[136,128]{1,0:T(8,128)S(1)}, f32[136,128]{1,0:T(8,128)S(1)}, u32[]{:S(2)}, u32[]{:S(2)}) %collective-permute-start.26) | collective-permute-done | bytes 69664 | tf_op jit(solution)/shard_map/ppermute | solution.py:269
  53.8 1.0 %finish.2 = (bf16[128,1024]{1,0:T(8,128)(2,1)}, f32[128,128]{1,0:T(8,128)S(1)}, s32[1]{0:T(128)}, s32[1]{0:T(128)}) custom-call(s32[1,100]{1,0:T(1,128)S(1)} %bitcast.13, f32[136,128]{1,0:T(8,128)S(1)} %get-tuple-element.136.refs_0_, f32[136,128]{1,0:T(8,128)S(1)} %collective-permute-done.25.refs_1_, f32[136,128]{1,0:T(8,128)S(1)} %collective-permute-done.26.refs_2_, ...), custom_call_target="tpu_custom_call" | custom-call | tf_op jit(solution)/shard_map/finish/pallas_call | solution.py:385
  (26 shorter events, 0.4 us)
Async XLA Ops:
  3.4 5.0 %collective-permute-start.14 = (bf16[32,640]{1,0:T(8,128)(2,1)S(1)}, bf16[32,640]{1,0:T(8,128)(2,1)S(1)}, u32[]{:S(2)}, u32[]{:S(2)}) collective-permute-start(bf16[32,640]{1,0:T(8,128)(2,1)S(1)} %get-tuple-element.123), channel_id=1, source_target_pairs={{0,2},{1,3},{2,0},{3,1},{4,6},{5,7},{6,4},{7,5},{8,10},{9,11},{10,... | collective-permute-start | bytes 122888 | tf_op jit(solution)/shard_map/ppermute | solution.py:269
  7.0 4.4 %collective-permute-start.15 = (bf16[32,640]{1,0:T(8,128)(2,1)S(1)}, bf16[32,640]{1,0:T(8,128)(2,1)S(1)}, u32[]{:S(2)}, u32[]{:S(2)}) collective-permute-start(bf16[32,640]{1,0:T(8,128)(2,1)S(1)} %get-tuple-element.123), channel_id=1, source_target_pairs={{0,3},{1,2},{2,1},{3,0},{4,7},{5,6},{6,5},{7,4},{8,11},{9,10},{10,... | collective-permute-start | bytes 122888 | tf_op jit(solution)/shard_map/ppermute | solution.py:269
  7.9 3.5 %collective-permute-start.16 = (bf16[32,640]{1,0:T(8,128)(2,1)S(1)}, bf16[32,640]{1,0:T(8,128)(2,1)S(1)}, u32[]{:S(2)}, u32[]{:S(2)}) collective-permute-start(bf16[32,640]{1,0:T(8,128)(2,1)S(1)} %get-tuple-element.123), channel_id=1, source_target_pairs={{0,1},{1,0},{2,3},{3,2},{4,5},{5,4},{6,7},{7,6},{8,9},{9,8},{10,11... | collective-permute-start | bytes 122888 | tf_op jit(solution)/shard_map/ppermute | solution.py:269
  11.4 8.1 %collective-permute-start.17 = (bf16[128,640]{1,0:T(8,128)(2,1)S(1)}, bf16[128,640]{1,0:T(8,128)(2,1)S(1)}, u32[]{:S(2)}, u32[]{:S(2)}) collective-permute-start(bf16[128,640]{1,0:T(8,128)(2,1)S(1)} %constant_dynamic-update-slice_fusion.4.refs_0_), channel_id=1, source_target_pairs={{0,28},{4,8},{8,4},{12,16},{16,12},{20,24},{24,20},{28,0},{1,29},{... | collective-permute-start | bytes 491528 | tf_op jit(solution)/shard_map/ppermute | solution.py:269
  16.8 4.5 %collective-permute-start.18 = (bf16[128,640]{1,0:T(8,128)(2,1)S(1)}, bf16[128,640]{1,0:T(8,128)(2,1)S(1)}, u32[]{:S(2)}, u32[]{:S(2)}) collective-permute-start(bf16[128,640]{1,0:T(8,128)(2,1)S(1)} %constant_dynamic-update-slice_fusion.4.refs_0_), channel_id=1, source_target_pairs={{0,4},{4,0},{8,12},{12,8},{16,20},{20,16},{24,28},{28,24},{1,5},{5... | collective-permute-start | bytes 491528 | tf_op jit(solution)/shard_map/ppermute | solution.py:269
  19.5 6.1 %collective-permute-start.20 = (bf16[128,640]{1,0:T(8,128)(2,1)S(1)}, bf16[128,640]{1,0:T(8,128)(2,1)S(1)}, u32[]{:S(2)}, u32[]{:S(2)}) collective-permute-start(bf16[128,640]{1,0:T(8,128)(2,1)S(1)} %collective-permute-done.17.refs_1_), channel_id=1, source_target_pairs={{0,4},{4,0},{8,12},{12,8},{16,20},{20,16},{24,28},{28,24},{1,5},{5... | collective-permute-start | bytes 491528 | tf_op jit(solution)/shard_map/ppermute | solution.py:269
  21.3 8.5 %collective-permute-start.19 = (bf16[128,640]{1,0:T(8,128)(2,1)S(1)}, bf16[128,640]{1,0:T(8,128)(2,1)S(1)}, u32[]{:S(2)}, u32[]{:S(2)}) collective-permute-start(bf16[128,640]{1,0:T(8,128)(2,1)S(1)} %collective-permute-done.18.refs_2_), channel_id=1, source_target_pairs={{0,28},{4,8},{8,4},{12,16},{16,12},{20,24},{24,20},{28,0},{1,29},{... | collective-permute-start | bytes 491528 | tf_op jit(solution)/shard_map/ppermute | solution.py:269
  25.6 6.9 %collective-permute-start.21 = (bf16[128,640]{1,0:T(8,128)(2,1)S(1)}, bf16[128,640]{1,0:T(8,128)(2,1)S(1)}, u32[]{:S(2)}, u32[]{:S(2)}) collective-permute-start(bf16[128,640]{1,0:T(8,128)(2,1)S(1)} %collective-permute-done.20.refs_4_), channel_id=1, source_target_pairs={{0,28},{4,8},{8,4},{12,16},{16,12},{20,24},{24,20},{28,0},{1,29},{... | collective-permute-start | bytes 491528 | tf_op jit(solution)/shard_map/ppermute | solution.py:269
  29.8 6.6 %collective-permute-start.22 = (bf16[128,640]{1,0:T(8,128)(2,1)S(1)}, bf16[128,640]{1,0:T(8,128)(2,1)S(1)}, u32[]{:S(2)}, u32[]{:S(2)}) collective-permute-start(bf16[128,640]{1,0:T(8,128)(2,1)S(1)} %collective-permute-done.19.refs_3_), channel_id=1, source_target_pairs={{0,4},{4,0},{8,12},{12,8},{16,20},{20,16},{24,28},{28,24},{1,5},{5... | collective-permute-start | bytes 491528 | tf_op jit(solution)/shard_map/ppermute | solution.py:269
  32.5 6.1 %collective-permute-start.23 = (bf16[128,640]{1,0:T(8,128)(2,1)S(1)}, bf16[128,640]{1,0:T(8,128)(2,1)S(1)}, u32[]{:S(2)}, u32[]{:S(2)}) collective-permute-start(bf16[128,640]{1,0:T(8,128)(2,1)S(1)} %collective-permute-done.21.refs_5_), channel_id=1, source_target_pairs={{0,4},{4,0},{8,12},{12,8},{16,20},{20,16},{24,28},{28,24},{1,5},{5... | collective-permute-start | bytes 491528 | tf_op jit(solution)/shard_map/ppermute | solution.py:269
  34.0 2.3 %copy-start = (s32[100]{0:T(128)S(1)}, s32[100]{0:T(128)}, u32[]{:S(2)}) copy-start(s32[100]{0:T(128)} %param.12) | copy-start | bytes 1204
  38.6 16.9 %copy-start.1 = (bf16[32,4096]{1,0:T(8,128)(2,1)S(1)}, bf16[32,4096]{1,0:T(8,128)(2,1)}, u32[]{:S(2)}) copy-start(bf16[32,4096]{1,0:T(8,128)(2,1)} %amp_ref.1) | copy-start | bytes 786436
  38.6 16.9 %copy-start.2 = (s32[2,4096]{1,0:T(2,128)S(1)}, s32[2,4096]{1,0:T(2,128)}, u32[]{:S(2)}) copy-start(s32[2,4096]{1,0:T(2,128)} %cd_ref.1) | copy-start | bytes 98308
  38.6 16.9 %copy-start.3 = (s32[1200]{0:T(1024)S(1)}, s32[1200]{0:T(1024)}, u32[]{:S(2)}) copy-start(s32[1200]{0:T(1024)} %vir_ref.1) | copy-start | bytes 14404
  39.2 7.3 %collective-permute-start.24 = (f32[4,136,128]{2,1,0:T(8,128)S(1)}, f32[4,136,128]{2,1,0:T(8,128)S(1)}, u32[]{:S(2)}, u32[]{:S(2)}) collective-permute-start(f32[4,136,128]{2,1,0:T(8,128)S(1)} %get-tuple-element.135), channel_id=1, source_target_pairs={{0,32},{32,0},{1,33},{33,1},{2,34},{34,2},{3,35},{35,3},{4,36},{36... | collective-permute-start | bytes 835592 | tf_op jit(solution)/shard_map/ppermute | solution.py:269
  46.5 4.8 %collective-permute-start.25 = (f32[136,128]{1,0:T(8,128)S(1)}, f32[136,128]{1,0:T(8,128)S(1)}, u32[]{:S(2)}, u32[]{:S(2)}) collective-permute-start(f32[136,128]{1,0:T(8,128)S(1)} %get-tuple-element.137), channel_id=1, source_target_pairs={{0,128},{64,192},{128,0},{192,64},{1,129},{65,193},{129,1},{193,65... | collective-permute-start | bytes 208904 | tf_op jit(solution)/shard_map/ppermute | solution.py:269
  49.5 4.4 %collective-permute-start.26 = (f32[136,128]{1,0:T(8,128)S(1)}, f32[136,128]{1,0:T(8,128)S(1)}, u32[]{:S(2)}, u32[]{:S(2)}) collective-permute-start(f32[136,128]{1,0:T(8,128)S(1)} %get-tuple-element.138), channel_id=1, source_target_pairs={{0,192},{64,128},{128,64},{192,0},{1,193},{65,129},{129,65},{193,1... | collective-permute-start | bytes 208904 | tf_op jit(solution)/shard_map/ppermute | solution.py:269
  50.2 3.6 %collective-permute-start.27 = (f32[136,128]{1,0:T(8,128)S(1)}, f32[136,128]{1,0:T(8,128)S(1)}, u32[]{:S(2)}, u32[]{:S(2)}) collective-permute-start(f32[136,128]{1,0:T(8,128)S(1)} %get-tuple-element.139), channel_id=1, source_target_pairs={{0,64},{64,0},{128,192},{192,128},{1,65},{65,1},{129,193},{193,129... | collective-permute-start | bytes 208904 | tf_op jit(solution)/shard_map/ppermute | solution.py:269

commit v2 on v1

--- a/solution.py
+++ b/solution.py
@@ -216,16 +216,19 @@
     keep_ref, send_ref, sums_s, occ_s = refs[-4:]
     multiply(n_occ, places, occ_ref, refs[:n], refs[n:-4], sums_s, occ_s)
     core, z = lax.axis_index("core"), lax.axis_index("z")
-    late = (z + 4) % 8
+    sign = 2 * (z % 2) - 1
+    late = [(z + dz * sign + 8) % 8 for dz, _ in places]
     for ref, odd in ((keep_ref, core), (send_ref, 1 - core)):
         for k in range(4):
             owner = 2 * k + odd
 
-            @pl.when(owner != late)
+            is_late = functools.reduce(jnp.logical_or, [owner == at for at in late])
+
+            @pl.when(jnp.logical_not(is_late))
             def _():
                 ref[k, :128] = early_ref[owner]
 
-            @pl.when(owner == late)
+            @pl.when(is_late)
             def _():
                 ref[k, :128] = sums_s[owner]
 
@@ -348,25 +351,25 @@
 
     sums = sds((8, 128, LANES), F32)
     early = pl.pallas_call(
-        functools.partial(early_kernel, n_occ, places[:-1]),
+        functools.partial(early_kernel, n_occ, places[:-2]),
         out_shape=sums,
-        in_specs=[VMEM] * (len(blocks) + len(parts)),
+        in_specs=[VMEM] * (len(blocks) - 1 + len(parts)),
         out_specs=VMEM,
         scratch_shapes=[pltpu.VMEM((1, LANES), I32)],
         compiler_params=params(8),
-        cost_estimate=cost(2 * 896 * cols * SLOTS, 4 << 20),
+        cost_estimate=cost(2 * 768 * cols * SLOTS, 4 << 20),
         name="early",
-    )(occ, *blocks[:-1], *parts)
+    )(occ, *blocks[:-2], *parts)
     keep, send = pl.pallas_call(
-        functools.partial(product_kernel, n_occ, places[-1:]),
+        functools.partial(product_kernel, n_occ, places[-2:]),
         out_shape=(sds((4, 136, LANES), F32),) * 2,
-        in_specs=[VMEM] * (4 + len(parts)),
+        in_specs=[VMEM] * (5 + len(parts)),
         out_specs=(VMEM,) * 2,
         scratch_shapes=[pltpu.VMEM((8, 128, LANES), F32), pltpu.VMEM((1, LANES), I32)],
         compiler_params=params(8),
-        cost_estimate=cost(2 * 128 * cols * SLOTS, 1 << 20),
+        cost_estimate=cost(2 * 256 * cols * SLOTS, 1 << 20),
         name="product",
-    )(occ, most, early, blocks[-1], *parts)
+    )(occ, most, early, *blocks[-2:], *parts)
 
     got = swap(send, "core", beside)
     folded = pl.pallas_call(

time: 56 us -> 54.7 us (0.977)
  waiting for transfers between devices: 12.7 us -> 11.9 us
    ppermute x14, waiting for transfers between devices: 12.7 us -> 11.9 us  [swap(): return lax.ppermute(a, axis, pairs)]
  transfers between devices with their start and end apart: 14 -> 14, of which waited for: 7 -> 8; matrix products, arithmetic and copies ran while one was open for 0% -> 0% of each run, Pallas kernels for 23% -> 23%
where the time goes in v2:
time: 54.7 us; the launch traced here: 54.6 us
  starting transfers between devices  23.8 us (44%)
  Pallas kernels  17.6 us (32%)
  waiting for transfers between devices  11.9 us (22%)
  between operations  0.97 us (2%)
    ppermute x14, starting transfers between devices, swap(): return lax.ppermute(a, axis, pairs)  23.8 us
    ppermute x14, waiting for transfers between devices, swap(): return lax.ppermute(a, axis, pairs)  11.9 us
    pallas_call x4, Pallas kernels, round_body(): pl.pallas_call(kernel, out_shape=out, in_specs=[SMEM, VMEM, VMEM, VMEM] +...  10.7 us
    pallas_call x1, Pallas kernels, round_body(): pl.pallas_call(functools.partial(pack_kernel, n_occ, n_vir), out_shape=(s...  3.38 us
    pallas_call x1, Pallas kernels, round_body(): pl.pallas_call(functools.partial(early_kernel, n_occ, places[:-2]), out_s...  1.88 us
  transfers between devices with their start and end apart: 14, of which 8 were waited for; matrix products, arithmetic and copies ran while one was open for 0% of the time, Pallas kernels for 23%

profile of v2, /device:TPU:1, one launch (start us, length us, event | category | flops | bytes accessed | tf_op | source)
XLA Modules:
  0.0 54.6 jit_solution(10877205581752599983)
XLA Ops:
  0.0 3.4 %pack.2 = (bf16[32,640]{1,0:T(8,128)(2,1)S(1)}, bf16[4,256,1024]{2,1,0:T(8,128)(2,1)S(1)}, s32[32,128]{1,0:T(8,128)S(1)}, f32[128,128]{1,0:T(8,128)S(1)}, f32[8,128]{1,0:T(8,128)S(1)}, /*index=5*/s32[8]{0:T(128)S(1)}) custom-call(s32[1]{0:T(128)} %constant.4.clone.1.start, s32[1,100]{1,0:T(1,128)} %bitcast.10, s32[1200]{0:T(1024)} %vir_ref.1, ...), custom_call_target="tpu_custom_call" | custom-call | flops 167772160 | bytes 6291456 | tf_op jit(solution)/shard_map/pack/pallas_call | solution.py:289
  3.4 3.7 %collective-permute-start.14 = (bf16[32,640]{1,0:T(8,128)(2,1)S(1)}, bf16[32,640]{1,0:T(8,128)(2,1)S(1)}, u32[]{:S(2)}, u32[]{:S(2)}) collective-permute-start(bf16[32,640]{1,0:T(8,128)(2,1)S(1)} %get-tuple-element.123), channel_id=1, source_target_pairs={{0,2},{1,3},{2,0},{3,1},{4,6},{5,7},{6,4},{7,5},{8,10},{9,11},{10,... | collective-permute-start | bytes 122888 | tf_op jit(solution)/shard_map/ppermute | solution.py:272
  7.0 0.9 %collective-permute-start.15 = (bf16[32,640]{1,0:T(8,128)(2,1)S(1)}, bf16[32,640]{1,0:T(8,128)(2,1)S(1)}, u32[]{:S(2)}, u32[]{:S(2)}) collective-permute-start(bf16[32,640]{1,0:T(8,128)(2,1)S(1)} %get-tuple-element.123), channel_id=1, source_target_pairs={{0,3},{1,2},{2,1},{3,0},{4,7},{5,6},{6,5},{7,4},{8,11},{9,10},{10,... | collective-permute-start | bytes 122888 | tf_op jit(solution)/shard_map/ppermute | solution.py:272
  7.9 0.5 collective-permute-done.14
  8.4 3.0 %collective-permute-done.15 = bf16[32,640]{1,0:T(8,128)(2,1)S(1)} collective-permute-done((bf16[32,640]{1,0:T(8,128)(2,1)S(1)}, bf16[32,640]{1,0:T(8,128)(2,1)S(1)}, u32[]{:S(2)}, u32[]{:S(2)}) %collective-permute-start.15) | collective-permute-done | bytes 40992 | tf_op jit(solution)/shard_map/ppermute | solution.py:272
  11.4 5.4 %collective-permute-start.17 = (bf16[128,640]{1,0:T(8,128)(2,1)S(1)}, bf16[128,640]{1,0:T(8,128)(2,1)S(1)}, u32[]{:S(2)}, u32[]{:S(2)}) collective-permute-start(bf16[128,640]{1,0:T(8,128)(2,1)S(1)} %constant_dynamic-update-slice_fusion.4.refs_0_), channel_id=1, source_target_pairs={{0,28},{4,8},{8,4},{12,16},{16,12},{20,24},{24,20},{28,0},{1,29},{... | collective-permute-start | bytes 491528 | tf_op jit(solution)/shard_map/ppermute | solution.py:272
  16.8 2.7 %collective-permute-done.17.refs_1_ = bf16[128,640]{1,0:T(8,128)(2,1)S(1)} collective-permute-done((bf16[128,640]{1,0:T(8,128)(2,1)S(1)}, bf16[128,640]{1,0:T(8,128)(2,1)S(1)}, u32[]{:S(2)}, u32[]{:S(2)}) %collective-permute-start.17) | collective-permute-done | bytes 163872 | tf_op jit(solution)/shard_map/ppermute | solution.py:272
  19.5 3.4 %weights.8 = (bf16[640,256]{1,0:T(8,128)(2,1)S(1)}, bf16[4096,256]{1,0:T(8,128)(2,1)S(1)}) custom-call(s32[8]{0:T(128)S(1)} %get-tuple-element.124.win, bf16[4,256,1024]{2,1,0:T(8,128)(2,1)S(1)} %get-tuple-element.125.hot_ref, s32[32,128]{1,0:T(8,128)S(1)} %get-tuple-element.126.slot_ref, f32[128,128]{1,0:T(8,128)S(1)} %get-tuple-element.127.symt_ref, ...), custom_call_target="tpu_custom_call" | custom-call | flops 1342177280 | bytes 7340032 | tf_op jit(solution)/shard_map/weights/pallas_call | solution.py:327
  22.9 2.8 %collective-permute-start.19 = (bf16[128,640]{1,0:T(8,128)(2,1)S(1)}, bf16[128,640]{1,0:T(8,128)(2,1)S(1)}, u32[]{:S(2)}, u32[]{:S(2)}) collective-permute-start(bf16[128,640]{1,0:T(8,128)(2,1)S(1)} %collective-permute-done.18.refs_2_), channel_id=1, source_target_pairs={{0,28},{4,8},{8,4},{12,16},{16,12},{20,24},{24,20},{28,0},{1,29},{... | collective-permute-start | bytes 491528 | tf_op jit(solution)/shard_map/ppermute | solution.py:272
  25.7 0.7 %collective-permute-start.21 = (bf16[128,640]{1,0:T(8,128)(2,1)S(1)}, bf16[128,640]{1,0:T(8,128)(2,1)S(1)}, u32[]{:S(2)}, u32[]{:S(2)}) collective-permute-start(bf16[128,640]{1,0:T(8,128)(2,1)S(1)} %collective-permute-done.20.refs_4_), channel_id=1, source_target_pairs={{0,28},{4,8},{8,4},{12,16},{16,12},{20,24},{24,20},{28,0},{1,29},{... | collective-permute-start | bytes 491528 | tf_op jit(solution)/shard_map/ppermute | solution.py:272
  26.3 2.3 %weights.9 = (bf16[640,256]{1,0:T(8,128)(2,1)S(1)}, bf16[4096,256]{1,0:T(8,128)(2,1)S(1)}) custom-call(s32[8]{0:T(128)S(1)} %get-tuple-element.124.win, bf16[4,256,1024]{2,1,0:T(8,128)(2,1)S(1)} %get-tuple-element.125.hot_ref, s32[32,128]{1,0:T(8,128)S(1)} %get-tuple-element.126.slot_ref, f32[128,128]{1,0:T(8,128)S(1)} %get-tuple-element.127.symt_ref, ...), custom_call_target="tpu_custom_call" | custom-call | flops 1342177280 | bytes 7340032 | tf_op jit(solution)/shard_map/weights/pallas_call | solution.py:327
  28.7 2.6 %weights.10 = (bf16[640,256]{1,0:T(8,128)(2,1)S(1)}, bf16[4096,256]{1,0:T(8,128)(2,1)S(1)}) custom-call(s32[8]{0:T(128)S(1)} %get-tuple-element.124.win, bf16[4,256,1024]{2,1,0:T(8,128)(2,1)S(1)} %get-tuple-element.125.hot_ref, s32[32,128]{1,0:T(8,128)S(1)} %get-tuple-element.126.slot_ref, f32[128,128]{1,0:T(8,128)S(1)} %get-tuple-element.127.symt_ref, ...), custom_call_target="tpu_custom_call" | custom-call | flops 1342177280 | bytes 7340032 | tf_op jit(solution)/shard_map/weights/pallas_call | solution.py:327
  31.5 0.7 %collective-permute-done.21.refs_5_ = bf16[128,640]{1,0:T(8,128)(2,1)S(1)} collective-permute-done((bf16[128,640]{1,0:T(8,128)(2,1)S(1)}, bf16[128,640]{1,0:T(8,128)(2,1)S(1)}, u32[]{:S(2)}, u32[]{:S(2)}) %collective-permute-start.21) | collective-permute-done | bytes 163872 | tf_op jit(solution)/shard_map/ppermute | solution.py:272
  32.2 0.7 %collective-permute-start.23 = (bf16[128,640]{1,0:T(8,128)(2,1)S(1)}, bf16[128,640]{1,0:T(8,128)(2,1)S(1)}, u32[]{:S(2)}, u32[]{:S(2)}) collective-permute-start(bf16[128,640]{1,0:T(8,128)(2,1)S(1)} %collective-permute-done.21.refs_5_), channel_id=1, source_target_pairs={{0,4},{4,0},{8,12},{12,8},{16,20},{20,16},{24,28},{28,24},{1,5},{5... | collective-permute-start | bytes 491528 | tf_op jit(solution)/shard_map/ppermute | solution.py:272
  32.9 2.3 %weights.11.refs_9_.refs_5_ = bf16[640,256]{1,0:T(8,128)(2,1)S(1)} custom-call(s32[8]{0:T(128)S(1)} %get-tuple-element.124.win, bf16[4,256,1024]{2,1,0:T(8,128)(2,1)S(1)} %get-tuple-element.125.hot_ref, s32[32,128]{1,0:T(8,128)S(1)} %get-tuple-element.126.slot_ref, f32[128,128]{1,0:T(8,128)S(1)} %get-tuple-element.127.symt_ref, ...), custom_call_target="tpu_custom_call" | custom-call | flops 1342177280 | bytes 7340032 | tf_op jit(solution)/shard_map/weights/pallas_call | solution.py:327
  35.2 1.9 %early.2.early_ref = f32[8,128,128]{2,1,0:T(8,128)S(1)} custom-call(s32[1,100]{1,0:T(1,128)S(1)} %bitcast.11, bf16[128,640]{1,0:T(8,128)(2,1)S(1)} %constant_dynamic-update-slice_fusion.4.refs_0_, bf16[128,640]{1,0:T(8,128)(2,1)S(1)} %collective-permute-done.17.refs_1_, bf16[128,640]{1,0:T(8,128)(2,1)S(1)} %collective-permute-done.18.refs_2_, ...), custom_call_target="tpu_custom_call" | custom-call | flops 1006632960 | bytes 4194304 | tf_op jit(solution)/shard_map/early/pallas_call | solution.py:353
  37.3 0.7 %product.2 = (f32[4,136,128]{2,1,0:T(8,128)S(1)}, f32[4,136,128]{2,1,0:T(8,128)S(1)}) custom-call(s32[1,100]{1,0:T(1,128)S(1)} %bitcast.12, f32[8,128]{1,0:T(8,128)S(1)} %get-tuple-element.122.cnt_ref, f32[8,128,128]{2,1,0:T(8,128)S(1)} %early.2.early_ref, bf16[128,640]{1,0:T(8,128)(2,1)S(1)} %collective-permute-done.22.refs_0_, ...), custom_call_target="tpu_custom_call" | custom-call | flops 335544320 | bytes 1048576 | tf_op jit(solution)/shard_map/product/pallas_call | solution.py:363
  38.1 5.9 %collective-permute-start.24 = (f32[4,136,128]{2,1,0:T(8,128)S(1)}, f32[4,136,128]{2,1,0:T(8,128)S(1)}, u32[]{:S(2)}, u32[]{:S(2)}) collective-permute-start(f32[4,136,128]{2,1,0:T(8,128)S(1)} %get-tuple-element.135), channel_id=1, source_target_pairs={{0,32},{32,0},{1,33},{33,1},{2,34},{34,2},{3,35},{35,3},{4,36},{36... | collective-permute-start | bytes 835592 | tf_op jit(solution)/shard_map/ppermute | solution.py:272
  44.0 1.2 %collective-permute-done.24.got_ref = f32[4,136,128]{2,1,0:T(8,128)S(1)} collective-permute-done((f32[4,136,128]{2,1,0:T(8,128)S(1)}, f32[4,136,128]{2,1,0:T(8,128)S(1)}, u32[]{:S(2)}, u32[]{:S(2)}) %collective-permute-start.24) | collective-permute-done | bytes 278560 | tf_op jit(solution)/shard_map/ppermute | solution.py:272
  45.2 3.0 %collective-permute-start.25 = (f32[136,128]{1,0:T(8,128)S(1)}, f32[136,128]{1,0:T(8,128)S(1)}, u32[]{:S(2)}, u32[]{:S(2)}) collective-permute-start(f32[136,128]{1,0:T(8,128)S(1)} %get-tuple-element.137), channel_id=1, source_target_pairs={{0,128},{64,192},{128,0},{192,64},{1,129},{65,193},{129,1},{193,65... | collective-permute-start | bytes 208904 | tf_op jit(solution)/shard_map/ppermute | solution.py:272
  48.2 0.8 %collective-permute-start.26 = (f32[136,128]{1,0:T(8,128)S(1)}, f32[136,128]{1,0:T(8,128)S(1)}, u32[]{:S(2)}, u32[]{:S(2)}) collective-permute-start(f32[136,128]{1,0:T(8,128)S(1)} %get-tuple-element.138), channel_id=1, source_target_pairs={{0,192},{64,128},{128,64},{192,0},{1,193},{65,129},{129,65},{193,1... | collective-permute-start | bytes 208904 | tf_op jit(solution)/shard_map/ppermute | solution.py:272
  49.0 1.0 %collective-permute-done.25.refs_1_ = f32[136,128]{1,0:T(8,128)S(1)} collective-permute-done((f32[136,128]{1,0:T(8,128)S(1)}, f32[136,128]{1,0:T(8,128)S(1)}, u32[]{:S(2)}, u32[]{:S(2)}) %collective-permute-start.25) | collective-permute-done | bytes 69664 | tf_op jit(solution)/shard_map/ppermute | solution.py:272
  50.0 2.6 %collective-permute-done.26.refs_2_ = f32[136,128]{1,0:T(8,128)S(1)} collective-permute-done((f32[136,128]{1,0:T(8,128)S(1)}, f32[136,128]{1,0:T(8,128)S(1)}, u32[]{:S(2)}, u32[]{:S(2)}) %collective-permute-start.26) | collective-permute-done | bytes 69664 | tf_op jit(solution)/shard_map/ppermute | solution.py:272
  52.6 1.0 %finish.2 = (bf16[128,1024]{1,0:T(8,128)(2,1)}, f32[128,128]{1,0:T(8,128)S(1)}, s32[1]{0:T(128)}, s32[1]{0:T(128)}) custom-call(s32[1,100]{1,0:T(1,128)S(1)} %bitcast.13, f32[136,128]{1,0:T(8,128)S(1)} %get-tuple-element.136.refs_0_, f32[136,128]{1,0:T(8,128)S(1)} %collective-permute-done.25.refs_1_, f32[136,128]{1,0:T(8,128)S(1)} %collective-permute-done.26.refs_2_, ...), custom_call_target="tpu_custom_call" | custom-call | tf_op jit(solution)/shard_map/finish/pallas_call | solution.py:388
  (26 shorter events, 0.7 us)
Async XLA Ops:
  3.4 5.0 %collective-permute-start.14 = (bf16[32,640]{1,0:T(8,128)(2,1)S(1)}, bf16[32,640]{1,0:T(8,128)(2,1)S(1)}, u32[]{:S(2)}, u32[]{:S(2)}) collective-permute-start(bf16[32,640]{1,0:T(8,128)(2,1)S(1)} %get-tuple-element.123), channel_id=1, source_target_pairs={{0,2},{1,3},{2,0},{3,1},{4,6},{5,7},{6,4},{7,5},{8,10},{9,11},{10,... | collective-permute-start | bytes 122888 | tf_op jit(solution)/shard_map/ppermute | solution.py:272
  7.0 4.4 %collective-permute-start.15 = (bf16[32,640]{1,0:T(8,128)(2,1)S(1)}, bf16[32,640]{1,0:T(8,128)(2,1)S(1)}, u32[]{:S(2)}, u32[]{:S(2)}) collective-permute-start(bf16[32,640]{1,0:T(8,128)(2,1)S(1)} %get-tuple-element.123), channel_id=1, source_target_pairs={{0,3},{1,2},{2,1},{3,0},{4,7},{5,6},{6,5},{7,4},{8,11},{9,10},{10,... | collective-permute-start | bytes 122888 | tf_op jit(solution)/shard_map/ppermute | solution.py:272
  7.9 3.5 %collective-permute-start.16 = (bf16[32,640]{1,0:T(8,128)(2,1)S(1)}, bf16[32,640]{1,0:T(8,128)(2,1)S(1)}, u32[]{:S(2)}, u32[]{:S(2)}) collective-permute-start(bf16[32,640]{1,0:T(8,128)(2,1)S(1)} %get-tuple-element.123), channel_id=1, source_target_pairs={{0,1},{1,0},{2,3},{3,2},{4,5},{5,4},{6,7},{7,6},{8,9},{9,8},{10,11... | collective-permute-start | bytes 122888 | tf_op jit(solution)/shard_map/ppermute | solution.py:272
  11.4 8.1 %collective-permute-start.17 = (bf16[128,640]{1,0:T(8,128)(2,1)S(1)}, bf16[128,640]{1,0:T(8,128)(2,1)S(1)}, u32[]{:S(2)}, u32[]{:S(2)}) collective-permute-start(bf16[128,640]{1,0:T(8,128)(2,1)S(1)} %constant_dynamic-update-slice_fusion.4.refs_0_), channel_id=1, source_target_pairs={{0,28},{4,8},{8,4},{12,16},{16,12},{20,24},{24,20},{28,0},{1,29},{... | collective-permute-start | bytes 491528 | tf_op jit(solution)/shard_map/ppermute | solution.py:272
  16.8 6.1 %collective-permute-start.18 = (bf16[128,640]{1,0:T(8,128)(2,1)S(1)}, bf16[128,640]{1,0:T(8,128)(2,1)S(1)}, u32[]{:S(2)}, u32[]{:S(2)}) collective-permute-start(bf16[128,640]{1,0:T(8,128)(2,1)S(1)} %constant_dynamic-update-slice_fusion.4.refs_0_), channel_id=1, source_target_pairs={{0,4},{4,0},{8,12},{12,8},{16,20},{20,16},{24,28},{28,24},{1,5},{5... | collective-permute-start | bytes 491528 | tf_op jit(solution)/shard_map/ppermute | solution.py:272
  19.5 6.2 %collective-permute-start.20 = (bf16[128,640]{1,0:T(8,128)(2,1)S(1)}, bf16[128,640]{1,0:T(8,128)(2,1)S(1)}, u32[]{:S(2)}, u32[]{:S(2)}) collective-permute-start(bf16[128,640]{1,0:T(8,128)(2,1)S(1)} %collective-permute-done.17.refs_1_), channel_id=1, source_target_pairs={{0,4},{4,0},{8,12},{12,8},{16,20},{20,16},{24,28},{28,24},{1,5},{5... | collective-permute-start | bytes 491528 | tf_op jit(solution)/shard_map/ppermute | solution.py:272
  22.9 8.4 %collective-permute-start.19 = (bf16[128,640]{1,0:T(8,128)(2,1)S(1)}, bf16[128,640]{1,0:T(8,128)(2,1)S(1)}, u32[]{:S(2)}, u32[]{:S(2)}) collective-permute-start(bf16[128,640]{1,0:T(8,128)(2,1)S(1)} %collective-permute-done.18.refs_2_), channel_id=1, source_target_pairs={{0,28},{4,8},{8,4},{12,16},{16,12},{20,24},{24,20},{28,0},{1,29},{... | collective-permute-start | bytes 491528 | tf_op jit(solution)/shard_map/ppermute | solution.py:272
  25.7 6.5 %collective-permute-start.21 = (bf16[128,640]{1,0:T(8,128)(2,1)S(1)}, bf16[128,640]{1,0:T(8,128)(2,1)S(1)}, u32[]{:S(2)}, u32[]{:S(2)}) collective-permute-start(bf16[128,640]{1,0:T(8,128)(2,1)S(1)} %collective-permute-done.20.refs_4_), channel_id=1, source_target_pairs={{0,28},{4,8},{8,4},{12,16},{16,12},{20,24},{24,20},{28,0},{1,29},{... | collective-permute-start | bytes 491528 | tf_op jit(solution)/shard_map/ppermute | solution.py:272
  31.3 5.8 %collective-permute-start.22 = (bf16[128,640]{1,0:T(8,128)(2,1)S(1)}, bf16[128,640]{1,0:T(8,128)(2,1)S(1)}, u32[]{:S(2)}, u32[]{:S(2)}) collective-permute-start(bf16[128,640]{1,0:T(8,128)(2,1)S(1)} %collective-permute-done.19.refs_3_), channel_id=1, source_target_pairs={{0,4},{4,0},{8,12},{12,8},{16,20},{20,16},{24,28},{28,24},{1,5},{5... | collective-permute-start | bytes 491528 | tf_op jit(solution)/shard_map/ppermute | solution.py:272
  32.2 5.1 %collective-permute-start.23 = (bf16[128,640]{1,0:T(8,128)(2,1)S(1)}, bf16[128,640]{1,0:T(8,128)(2,1)S(1)}, u32[]{:S(2)}, u32[]{:S(2)}) collective-permute-start(bf16[128,640]{1,0:T(8,128)(2,1)S(1)} %collective-permute-done.21.refs_5_), channel_id=1, source_target_pairs={{0,4},{4,0},{8,12},{12,8},{16,20},{20,16},{24,28},{28,24},{1,5},{5... | collective-permute-start | bytes 491528 | tf_op jit(solution)/shard_map/ppermute | solution.py:272
  32.9 2.3 %copy-start = (s32[100]{0:T(128)S(1)}, s32[100]{0:T(128)}, u32[]{:S(2)}) copy-start(s32[100]{0:T(128)} %param.12) | copy-start | bytes 1204
  37.1 17.1 %copy-start.1 = (bf16[32,4096]{1,0:T(8,128)(2,1)S(1)}, bf16[32,4096]{1,0:T(8,128)(2,1)}, u32[]{:S(2)}) copy-start(bf16[32,4096]{1,0:T(8,128)(2,1)} %amp_ref.1) | copy-start | bytes 786436
  37.1 17.1 %copy-start.2 = (s32[2,4096]{1,0:T(2,128)S(1)}, s32[2,4096]{1,0:T(2,128)}, u32[]{:S(2)}) copy-start(s32[2,4096]{1,0:T(2,128)} %cd_ref.1) | copy-start | bytes 98308
  37.1 17.1 %copy-start.3 = (s32[1200]{0:T(1024)S(1)}, s32[1200]{0:T(1024)}, u32[]{:S(2)}) copy-start(s32[1200]{0:T(1024)} %vir_ref.1) | copy-start | bytes 14404
  38.1 7.1 %collective-permute-start.24 = (f32[4,136,128]{2,1,0:T(8,128)S(1)}, f32[4,136,128]{2,1,0:T(8,128)S(1)}, u32[]{:S(2)}, u32[]{:S(2)}) collective-permute-start(f32[4,136,128]{2,1,0:T(8,128)S(1)} %get-tuple-element.135), channel_id=1, source_target_pairs={{0,32},{32,0},{1,33},{33,1},{2,34},{34,2},{3,35},{35,3},{4,36},{36... | collective-permute-start | bytes 835592 | tf_op jit(solution)/shard_map/ppermute | solution.py:272
  45.2 4.8 %collective-permute-start.25 = (f32[136,128]{1,0:T(8,128)S(1)}, f32[136,128]{1,0:T(8,128)S(1)}, u32[]{:S(2)}, u32[]{:S(2)}) collective-permute-start(f32[136,128]{1,0:T(8,128)S(1)} %get-tuple-element.137), channel_id=1, source_target_pairs={{0,128},{64,192},{128,0},{192,64},{1,129},{65,193},{129,1},{193,65... | collective-permute-start | bytes 208904 | tf_op jit(solution)/shard_map/ppermute | solution.py:272
  48.2 4.4 %collective-permute-start.26 = (f32[136,128]{1,0:T(8,128)S(1)}, f32[136,128]{1,0:T(8,128)S(1)}, u32[]{:S(2)}, u32[]{:S(2)}) collective-permute-start(f32[136,128]{1,0:T(8,128)S(1)} %get-tuple-element.138), channel_id=1, source_target_pairs={{0,192},{64,128},{128,64},{192,0},{1,193},{65,129},{129,65},{193,1... | collective-permute-start | bytes 208904 | tf_op jit(solution)/shard_map/ppermute | solution.py:272
  49.0 3.6 %collective-permute-start.27 = (f32[136,128]{1,0:T(8,128)S(1)}, f32[136,128]{1,0:T(8,128)S(1)}, u32[]{:S(2)}, u32[]{:S(2)}) collective-permute-start(f32[136,128]{1,0:T(8,128)S(1)} %get-tuple-element.139), channel_id=1, source_target_pairs={{0,64},{64,0},{128,192},{192,128},{1,65},{65,1},{129,193},{193,129... | collective-permute-start | bytes 208904 | tf_op jit(solution)/shard_map/ppermute | solution.py:272
